TPU v7x, 512 devices: a whole 4x4x16 slice. The times are simulated.
512 devices in a mesh: dp: 8 (over z_hi, y), shard: 64 (over x, z_lo, core).
Axes of the slice: x: 4, y: 4, z: 16 (z_hi: 2, z_lo: 8; z = z_hi * 8 + z_lo), core: 2. Of those that a mesh axis runs over, the one named last changes fastest.
Arguments:
- context: bfloat16 [8192, 4096], P('shard'), may hold values from -16 to 16
- projected: bfloat16 [8192, 4096], P('shard', 'dp'), may hold values from -6 to 6
- cotangent: bfloat16 [8192, 4096], P('shard', 'dp'), may hold values from -16 to 16
- modality: int32 [8192], P('shard'), may hold values from 0 to 2
- out_weight: bfloat16 [4096, 3, 4096], P('shard', None, 'dp'), may hold values from -0.09375 to 0.09375
- out_gain: float32 [3, 4096], P(None, 'dp'), may hold values from 0.25 to 1.75
Outputs:
- grad_context: bfloat16 [8192, 4096], P('shard', 'dp')
- grad_weight: float32 [4096, 3, 4096], P('shard', None, 'dp')
- grad_gain: float32 [3, 4096], P(None, 'dp')
All inputs are finite; a program needn't handle non-finite values.
Results may differ from a plain program's by a relative error of at most 0.0049.
Values may be sent and summed in bfloat16 or wider, within the bound.
No kernel may reach another device: no remote copies, remote signals or barrier semaphores. Data moves between devices by JAX's collectives and lax.ppermute only.
A program may use at most 64 MiB of HBM per device.

v0:
```python
import jax
import jax.numpy as jnp
from jax import lax
from jax.sharding import Mesh
from jax.sharding import PartitionSpec as P


DP = ("zi", "y")
SHARD = ("x", "zh", "zl", "c")
GROUP = ("zl", "c")

EPS = 1e-06
F32 = jnp.float32
BF16 = jnp.bfloat16


def swap(value, axis):
    return lax.ppermute(value, axis, [(0, 1), (1, 0)])


def crossed(value, axis, k):
    return lax.ppermute(value, axis, [(i, i ^ k) for i in range(lax.axis_size(axis))])


def two_terms(value):
    high = lax.reduce_precision(value, 8, 7)
    return jnp.concatenate([high, value - high], axis=0).astype(BF16)


def joined_terms(rows, count):
    rows = rows.astype(F32)
    return rows[..., :count, :] + rows[..., count : 2 * count, :]


def in_order(index, own, other, axis):
    first = jnp.where(index == 0, own, other)
    second = jnp.where(index == 0, other, own)
    return jnp.stack([first, second], axis=axis)


def local(context, projected, cotangent, modality, out_weight, out_gain):
    tok, feats = context.shape
    rows, towers, cols = out_weight.shape
    width = cols * lax.axis_size(DP)
    xs, ys = lax.axis_size("x"), lax.axis_size("y")
    members = lax.axis_size(GROUP)
    x, zh, c, zi = (lax.axis_index(a) for a in ("x", "zh", "c", "zi"))
    blocks = feats // (members * rows)

    feature_rows = context.reshape(tok, blocks, members, rows).transpose(2, 0, 1, 3)
    feature_rows = feature_rows.reshape(members, tok, blocks * rows)
    ctx = lax.all_to_all(feature_rows, GROUP, 0, 0, tiled=True)
    ctx = ctx.reshape(members * tok, blocks * rows)

    weight = out_weight.transpose(1, 0, 2)
    other = swap(weight, "zh")
    pair = in_order(zh, weight, other, 1)
    every = jnp.zeros((towers, 2, 2, xs // 2, rows, cols), BF16)
    for k in range(xs):
        source = x ^ k
        piece = pair if k == 0 else crossed(pair, "x", k)
        every = lax.dynamic_update_slice(
            every, piece[:, None, :, None], (0, source & 1, 0, source >> 1, 0, 0)
        )
    every = every.reshape(towers, blocks * rows, cols)

    onehot = (modality[:, None] == jnp.arange(towers, dtype=jnp.int32)[None, :]).astype(F32)
    proj_float = projected.astype(F32)
    cot_float = cotangent.astype(F32)
    gain_tok = jnp.dot(onehot, out_gain, precision=lax.Precision.HIGHEST)
    scaled = cot_float * gain_tok
    stats = jnp.stack(
        [jnp.sum(proj_float * proj_float, axis=1), jnp.sum(scaled * proj_float, axis=1)]
    )
    stats = lax.all_gather(stats, "y")
    stats = jnp.sum(stats, axis=0)
    stats = stats + swap(stats, "zi")
    inverse_rms = lax.rsqrt(stats[0] / width + EPS)[:, None]
    inner = inverse_rms * stats[1][:, None]
    normed = proj_float * inverse_rms
    gain_terms = jnp.dot(onehot.T, cot_float * normed, precision=lax.Precision.HIGHEST)
    grad_proj = (inverse_rms * (scaled - normed * (inner / width))).astype(BF16)

    spare = 16 - 2 * towers - 1
    mod_row = jnp.pad(modality.astype(BF16), (0, cols - tok))[None]
    packet = jnp.concatenate(
        [grad_proj, two_terms(gain_terms), mod_row, jnp.zeros((spare, cols), BF16)], axis=0
    )
    line = lax.axis_size("zl")
    packets = jnp.broadcast_to(packet[None], (line, *packet.shape))
    packets = lax.all_to_all(packets, "zl", 0, 0, tiled=True)
    packets = in_order(c, packets, swap(packets, "c"), 1).reshape(members, tok + 16, cols)
    grads = packets[:, :tok].reshape(members * tok, cols)
    gain_part = jnp.sum(joined_terms(packets[:, tok:], towers), axis=0)
    ids = packets[:, tok + 2 * towers, :tok].astype(jnp.int32).reshape(members * tok)

    partial = jnp.zeros((blocks * rows, members * tok), F32)
    for m in range(towers):
        product = lax.dot_general(
            every[m], grads, (((1,), (1,)), ((), ())), preferred_element_type=F32
        )
        partial = partial + (ids == m).astype(F32)[None, :] * product
    partial = partial.astype(BF16).reshape(ys, 2 * rows, members * tok)
    partial = lax.all_to_all(partial, "y", 0, 0, tiled=True)
    partial = jnp.sum(partial.astype(F32), axis=0).reshape(2, rows, members * tok)
    kept = jnp.where(zi == 0, partial[0], partial[1])
    sent = jnp.where(zi == 0, partial[1], partial[0]).astype(BF16)
    got = swap(sent, "zi")
    total = (kept + got.astype(F32)).astype(BF16)
    total = total.reshape(rows, members, tok).transpose(1, 0, 2)
    settled = lax.all_to_all(total, GROUP, 0, 0, tiled=True)
    grad_context = settled.reshape(members * rows, tok).T

    updates = []
    for m in range(towers):
        masked = jnp.where((ids == m)[:, None], ctx, jnp.zeros_like(ctx))
        update = lax.dot_general(
            masked, grads, (((0,), (0,)), ((), ())), preferred_element_type=F32
        )
        updates.append(update.astype(BF16).reshape(xs, 2 * rows, cols))
    gain_rows = jnp.pad(two_terms(gain_part), ((0, 16 - 2 * towers), (0, 0)))
    updates.append(jnp.broadcast_to(gain_rows[None], (xs, 16, cols)))
    updates = jnp.concatenate(updates, axis=1)
    parts = []
    for k in range(xs):
        part = lax.dynamic_index_in_dim(updates, x ^ k, 0, keepdims=False)
        parts.append(part if k == 0 else crossed(part, "x", k))
    size = towers * 2 * rows
    weight_part = [part[:size].astype(F32) for part in parts]
    weight_part = (weight_part[0] + weight_part[1]) + (weight_part[2] + weight_part[3])
    weight_part = weight_part.reshape(towers, 2, rows, cols)
    gain_part = [joined_terms(part[size:], towers) for part in parts]
    gain_part = (gain_part[0] + gain_part[1]) + (gain_part[2] + gain_part[3])
    kept = jnp.where(zh == 0, weight_part[:, 0], weight_part[:, 1])
    sent = jnp.where(zh == 0, weight_part[:, 1], weight_part[:, 0]).astype(BF16)
    gain_rows = jnp.pad(two_terms(gain_part), ((0, 16 - 2 * towers), (0, 0)))
    sent = jnp.concatenate([sent.reshape(towers * rows, cols), gain_rows], axis=0)
    got = swap(sent, "zh")
    grad_weight = kept + got[: towers * rows].reshape(towers, rows, cols).astype(F32)
    grad_weight = grad_weight.transpose(1, 0, 2)
    grad_gain = joined_terms(gain_rows, towers) + joined_terms(got[towers * rows :], towers)
    return (grad_context, grad_weight, grad_gain)


def solution(mesh):
    finer = Mesh(mesh.devices.reshape(2, 4, 4, 2, 4, 2), DP + SHARD)

    return jax.shard_map(
        local,
        mesh=finer,
        in_specs=(
            P(SHARD, None),
            P(SHARD, DP),
            P(SHARD, DP),
            P(SHARD),
            P(SHARD, None, DP),
            P(None, DP),
        ),
        out_specs=(P(SHARD, DP), P(SHARD, None, DP), P(None, DP)),
        check_vma=False,
    )
```

profile of v0, /device:TPU:1, one launch (start us, length us, event | category | flops | bytes accessed | tf_op | source)
XLA Modules:
  0.0 216.7 jit_solution(15149560774950885258)
XLA Ops:
  0.6 0.7 copy-done
  1.3 1.4 fusion.19
  2.8 8.9 %all-gather.1 = f32[4,2,128]{2,1,0:T(2,128)S(1)} all-gather(f32[1,2,128]{2,1,0:T(2,128)S(1)} %maximum_bitcast_fusion), channel_id=2, replica_groups=mesh['zi'=2,'y'=4,'x'=4,'zh'=2,'zl'=4,'c'=2] {'y'}, dimensions={0}, use_global_device_ids=true | all-gather | bytes 5120 | tf_op jit(solution)/shard_map/all_gather | solution.py:75
  11.7 15.4 %collective-permute-start = (f32[2,128]{1,0:T(2,128)S(1)}, f32[2,128]{1,0:T(2,128)S(1)}, u32[]{:S(2)}, u32[]{:S(2)}) collective-permute-start(f32[2,128]{1,0:T(2,128)S(1)} %reduce_sum.47), channel_id=1, source_target_pairs={{0,256},{256,0},{1,257},{257,1},{2,258},{258,2},{3,259},{259,3},{4... | collective-permute-start | bytes 3080 | tf_op jit(solution)/shard_map/ppermute | solution.py:18
  27.1 0.7 convert_element_type.154
  27.8 0.3 collective-permute-done
  28.1 1.3 fusion.32
  29.4 1.0 fusion.17
  30.6 0.9 broadcast_in_dim.62
  31.5 3.5 %all-to-all-start = ((bf16[4,144,512]{2,1,0:T(8,128)(2,1)}), bf16[4,144,512]{2,1,0:T(8,128)(2,1)S(1)}, u32[]{:S(2)}, u32[]{:S(2)}) async-start(bf16[4,144,512]{2,1,0:T(8,128)(2,1)} %broadcast_in_dim.62), calls=%async_computation | async-start | bytes 1179648 | tf_op jit(solution)/shard_map/all_to_all | solution.py:91
  35.0 7.6 %collective-permute-start.2 = (bf16[3,64,512]{2,1,0:T(8,128)(2,1)S(1)}, bf16[3,64,512]{2,1,0:T(8,128)(2,1)S(1)}, u32[]{:S(2)}, u32[]{:S(2)}) collective-permute-start(bf16[3,64,512]{2,1,0:T(8,128)(2,1)S(1)} %bitcast.149), channel_id=1, source_target_pairs={{0,8},{8,0},{1,9},{9,1},{2,10},{10,2},{3,11},{11,3},{4,12},{12,4},... | collective-permute-start | bytes 589832 | tf_op jit(solution)/shard_map/ppermute | solution.py:18
  42.6 4.7 %collective-permute-done.2 = bf16[3,64,512]{2,1,0:T(8,128)(2,1)S(1)} collective-permute-done((bf16[3,64,512]{2,1,0:T(8,128)(2,1)S(1)}, bf16[3,64,512]{2,1,0:T(8,128)(2,1)S(1)}, u32[]{:S(2)}, u32[]{:S(2)}) %collective-permute-start.2) | collective-permute-done | bytes 196640 | tf_op jit(solution)/shard_map/ppermute | solution.py:18
  47.4 3.1 %collective-permute-start.3 = (bf16[3,2,64,512]{3,2,1,0:T(8,128)(2,1)S(1)}, bf16[3,2,64,512]{3,2,1,0:T(8,128)(2,1)}, u32[]{:S(2)}, u32[]{:S(2)}) collective-permute-start(bf16[3,2,64,512]{3,2,1,0:T(8,128)(2,1)S(1)} %pad_maximum_fusion.2), channel_id=1, source_target_pairs={{0,16},{16,0},{32,48},{48,32},{1,17},{17,1},{33,49},{49,33},{2,18}... | collective-permute-start | bytes 1179656 | tf_op jit(solution)/shard_map/ppermute | solution.py:22
  50.5 4.4 %collective-permute-start.4 = (bf16[3,2,64,512]{3,2,1,0:T(8,128)(2,1)S(1)}, bf16[3,2,64,512]{3,2,1,0:T(8,128)(2,1)S(1)}, u32[]{:S(2)}, u32[]{:S(2)}) collective-permute-start(bf16[3,2,64,512]{3,2,1,0:T(8,128)(2,1)S(1)} %pad_maximum_fusion.2), channel_id=1, source_target_pairs={{0,32},{16,48},{32,0},{48,16},{1,33},{17,49},{33,1},{49,17},{2,34}... | collective-permute-start | bytes 1179656 | tf_op jit(solution)/shard_map/ppermute | solution.py:22
  54.9 2.1 collective-permute-start.5
  57.2 1.0 bitcast_dynamic-update-slice_fusion.1
  58.3 9.8 %collective-permute-start.1 = (bf16[4,144,512]{2,1,0:T(8,128)(2,1)S(1)}, bf16[4,144,512]{2,1,0:T(8,128)(2,1)S(1)}, u32[]{:S(2)}, u32[]{:S(2)}) collective-permute-start(bf16[4,144,512]{2,1,0:T(8,128)(2,1)S(1)} %all-to-all-done), channel_id=1, source_target_pairs={{0,1},{1,0},{2,3},{3,2},{4,5},{5,4},{6,7},{7,6},{8,9},{9,8},{10,11... | collective-permute-start | bytes 1769480 | tf_op jit(solution)/shard_map/ppermute | solution.py:18
  68.1 4.3 %collective-permute-done.5 = bf16[3,2,64,512]{3,2,1,0:T(8,128)(2,1)} collective-permute-done((bf16[3,2,64,512]{3,2,1,0:T(8,128)(2,1)S(1)}, bf16[3,2,64,512]{3,2,1,0:T(8,128)(2,1)}, u32[]{:S(2)}, u32[]{:S(2)}) %collective-permute-start.5) | collective-permute-done | bytes 393248 | tf_op jit(solution)/shard_map/ppermute | solution.py:22
  72.4 1.0 bitcast_dynamic-update-slice_fusion.3
  73.9 0.7 fusion.54
  74.7 0.7 fusion.53
  75.4 1.8 add_convert_fusion
  77.2 3.5 %all-to-all-start.1 = ((bf16[4,128,1024]{2,1,0:T(8,128)(2,1)}), bf16[4,128,1024]{2,1,0:T(8,128)(2,1)S(1)}, u32[]{:S(2)}, u32[]{:S(2)}) async-start(bf16[4,128,1024]{2,1,0:T(8,128)(2,1)} %bitcast.27), calls=%async_computation.1 | async-start | bytes 2097152 | tf_op jit(solution)/shard_map/all_to_all | solution.py:104
  80.7 1.6 copy.40
  82.3 1.1 copy.41
  83.4 8.3 %all-to-all-done.1 = bf16[4,128,1024]{2,1,0:T(8,128)(2,1)S(1)} async-done(((bf16[4,128,1024]{2,1,0:T(8,128)(2,1)}), bf16[4,128,1024]{2,1,0:T(8,128)(2,1)S(1)}, u32[]{:S(2)}, u32[]{:S(2)}) %all-to-all-start.1) | async-done | bytes 1048608 | tf_op jit(solution)/shard_map/all_to_all | solution.py:104
  91.7 25.6 %all-to-all-start.3 = ((bf16[8,128,512]{1,2,0:T(8,128)(2,1)}), bf16[8,128,512]{1,2,0:T(8,128)(2,1)}, u32[]{:S(2)}, u32[]{:S(2)}) async-start(bf16[8,128,512]{1,2,0:T(8,128)(2,1)} %bitcast.33), calls=%async_computation.3 | async-start | bytes 2097152 | tf_op jit(solution)/shard_map/all_to_all | solution.py:52
  117.6 7.0 %collective-permute-start.6 = (bf16[64,1024]{1,0:T(8,128)(2,1)S(1)}, bf16[64,1024]{1,0:T(8,128)(2,1)S(1)}, u32[]{:S(2)}, u32[]{:S(2)}) collective-permute-start(bf16[64,1024]{1,0:T(8,128)(2,1)S(1)} %select_convert_fusion.1), channel_id=1, source_target_pairs={{0,256},{256,0},{1,257},{257,1},{2,258},{258,2},{3,259},{259,3},{4... | collective-permute-start | bytes 393224 | tf_op jit(solution)/shard_map/ppermute | solution.py:18
  124.7 26.7 %all-to-all-done.3 = bf16[8,128,512]{1,2,0:T(8,128)(2,1)} async-done(((bf16[8,128,512]{1,2,0:T(8,128)(2,1)}), bf16[8,128,512]{1,2,0:T(8,128)(2,1)}, u32[]{:S(2)}, u32[]{:S(2)}) %all-to-all-start.3) | async-done | bytes 1048608 | tf_op jit(solution)/shard_map/all_to_all | solution.py:52
  151.4 1.9 fusion.2
  153.3 1.9 fusion.1
  155.3 1.9 fusion
  157.4 0.8 dynamic-slice_bitcast_fusion.2
  158.2 1.9 collective-permute-start.7
  160.1 2.1 collective-permute-start.9
  162.3 4.9 %collective-permute-start.8 = (bf16[400,512]{1,0:T(8,128)(2,1)S(1)}, bf16[400,512]{1,0:T(8,128)(2,1)}, u32[]{:S(2)}, u32[]{:S(2)}) collective-permute-start(bf16[400,512]{1,0:T(8,128)(2,1)S(1)} %get-tuple-element.18), channel_id=1, source_target_pairs={{0,32},{16,48},{32,0},{48,16},{1,33},{17,49},{33,1},{49,17},{2,34}... | collective-permute-start | bytes 1228808 | tf_op jit(solution)/shard_map/ppermute | solution.py:22
  167.3 0.7 copy.39
  168.0 7.2 %all-to-all-start.2 = ((bf16[8,64,128]{2,1,0:T(8,128)(2,1)}), bf16[8,64,128]{2,1,0:T(8,128)(2,1)S(1)}, u32[]{:S(2)}, u32[]{:S(2)}) async-start(bf16[8,64,128]{2,1,0:T(8,128)(2,1)} %copy.39), calls=%async_computation.2 | async-start | bytes 262144 | tf_op jit(solution)/shard_map/all_to_all | solution.py:111
  175.2 7.0 %collective-permute-done.9 = bf16[400,512]{1,0:T(8,128)(2,1)} collective-permute-done((bf16[400,512]{1,0:T(8,128)(2,1)S(1)}, bf16[400,512]{1,0:T(8,128)(2,1)}, u32[]{:S(2)}, u32[]{:S(2)}) %collective-permute-start.9) | collective-permute-done | bytes 409632 | tf_op jit(solution)/shard_map/ppermute | solution.py:22
  182.2 1.4 fusion.9
  183.7 0.7 slice_convert_fusion.4
  184.4 0.7 slice_convert_fusion.2
  185.1 0.7 slice_convert_fusion.3
  185.9 11.0 %collective-permute-start.10 = (bf16[208,512]{1,0:T(8,128)(2,1)S(1)}, bf16[208,512]{1,0:T(8,128)(2,1)S(1)}, u32[]{:S(2)}, u32[]{:S(2)}) collective-permute-start(bf16[208,512]{1,0:T(8,128)(2,1)S(1)} %pad_maximum_fusion.3), channel_id=1, source_target_pairs={{0,8},{8,0},{1,9},{9,1},{2,10},{10,2},{3,11},{11,3},{4,12},{12,4},... | collective-permute-start | bytes 638984 | tf_op jit(solution)/shard_map/ppermute | solution.py:18
  196.9 0.8 copy.44
  197.7 17.6 %collective-permute-done.10 = bf16[208,512]{1,0:T(8,128)(2,1)S(1)} collective-permute-done((bf16[208,512]{1,0:T(8,128)(2,1)S(1)}, bf16[208,512]{1,0:T(8,128)(2,1)S(1)}, u32[]{:S(2)}, u32[]{:S(2)}) %collective-permute-start.10) | collective-permute-done | bytes 213024 | tf_op jit(solution)/shard_map/ppermute | solution.py:18
  215.2 0.8 fusion.13
  216.1 0.6 fusion.35
  (50 shorter events, 1.6 us)
Async XLA Ops:
  0.6 0.7 copy-start
  2.7 32.3 %copy-start.1 = (bf16[64,3,512]{2,0,1:T(8,128)(2,1)S(1)}, bf16[64,3,512]{2,0,1:T(8,128)(2,1)}, u32[]{:S(2)}) copy-start(bf16[64,3,512]{2,0,1:T(8,128)(2,1)} %param.10) | copy-start | bytes 589828
  11.7 16.4 %collective-permute-start = (f32[2,128]{1,0:T(2,128)S(1)}, f32[2,128]{1,0:T(2,128)S(1)}, u32[]{:S(2)}, u32[]{:S(2)}) collective-permute-start(f32[2,128]{1,0:T(2,128)S(1)} %reduce_sum.47), channel_id=1, source_target_pairs={{0,256},{256,0},{1,257},{257,1},{2,258},{258,2},{3,259},{259,3},{4... | collective-permute-start | bytes 3080 | tf_op jit(solution)/shard_map/ppermute | solution.py:18
  31.5 26.7 %all-to-all-start = ((bf16[4,144,512]{2,1,0:T(8,128)(2,1)}), bf16[4,144,512]{2,1,0:T(8,128)(2,1)S(1)}, u32[]{:S(2)}, u32[]{:S(2)}) async-start(bf16[4,144,512]{2,1,0:T(8,128)(2,1)} %broadcast_in_dim.62), calls=%async_computation | async-start | bytes 1179648 | tf_op jit(solution)/shard_map/all_to_all | solution.py:91
  35.0 12.3 %collective-permute-start.2 = (bf16[3,64,512]{2,1,0:T(8,128)(2,1)S(1)}, bf16[3,64,512]{2,1,0:T(8,128)(2,1)S(1)}, u32[]{:S(2)}, u32[]{:S(2)}) collective-permute-start(bf16[3,64,512]{2,1,0:T(8,128)(2,1)S(1)} %bitcast.149), channel_id=1, source_target_pairs={{0,8},{8,0},{1,9},{9,1},{2,10},{10,2},{3,11},{11,3},{4,12},{12,4},... | collective-permute-start | bytes 589832 | tf_op jit(solution)/shard_map/ppermute | solution.py:18
  47.4 9.9 %collective-permute-start.3 = (bf16[3,2,64,512]{3,2,1,0:T(8,128)(2,1)S(1)}, bf16[3,2,64,512]{3,2,1,0:T(8,128)(2,1)}, u32[]{:S(2)}, u32[]{:S(2)}) collective-permute-start(bf16[3,2,64,512]{3,2,1,0:T(8,128)(2,1)S(1)} %pad_maximum_fusion.2), channel_id=1, source_target_pairs={{0,16},{16,0},{32,48},{48,32},{1,17},{17,1},{33,49},{49,33},{2,18}... | collective-permute-start | bytes 1179656 | tf_op jit(solution)/shard_map/ppermute | solution.py:22
  50.5 17.6 %collective-permute-start.4 = (bf16[3,2,64,512]{3,2,1,0:T(8,128)(2,1)S(1)}, bf16[3,2,64,512]{3,2,1,0:T(8,128)(2,1)S(1)}, u32[]{:S(2)}, u32[]{:S(2)}) collective-permute-start(bf16[3,2,64,512]{3,2,1,0:T(8,128)(2,1)S(1)} %pad_maximum_fusion.2), channel_id=1, source_target_pairs={{0,32},{16,48},{32,0},{48,16},{1,33},{17,49},{33,1},{49,17},{2,34}... | collective-permute-start | bytes 1179656 | tf_op jit(solution)/shard_map/ppermute | solution.py:22
  54.9 17.5 %collective-permute-start.5 = (bf16[3,2,64,512]{3,2,1,0:T(8,128)(2,1)S(1)}, bf16[3,2,64,512]{3,2,1,0:T(8,128)(2,1)}, u32[]{:S(2)}, u32[]{:S(2)}) collective-permute-start(bf16[3,2,64,512]{3,2,1,0:T(8,128)(2,1)S(1)} %pad_maximum_fusion.2), channel_id=1, source_target_pairs={{0,48},{16,32},{32,16},{48,0},{1,49},{17,33},{33,17},{49,1},{2,50}... | collective-permute-start | bytes 1179656 | tf_op jit(solution)/shard_map/ppermute | solution.py:22
  58.3 15.3 %collective-permute-start.1 = (bf16[4,144,512]{2,1,0:T(8,128)(2,1)S(1)}, bf16[4,144,512]{2,1,0:T(8,128)(2,1)S(1)}, u32[]{:S(2)}, u32[]{:S(2)}) collective-permute-start(bf16[4,144,512]{2,1,0:T(8,128)(2,1)S(1)} %all-to-all-done), channel_id=1, source_target_pairs={{0,1},{1,0},{2,3},{3,2},{4,5},{5,4},{6,7},{7,6},{8,9},{9,8},{10,11... | collective-permute-start | bytes 1769480 | tf_op jit(solution)/shard_map/ppermute | solution.py:18
  77.2 14.5 %all-to-all-start.1 = ((bf16[4,128,1024]{2,1,0:T(8,128)(2,1)}), bf16[4,128,1024]{2,1,0:T(8,128)(2,1)S(1)}, u32[]{:S(2)}, u32[]{:S(2)}) async-start(bf16[4,128,1024]{2,1,0:T(8,128)(2,1)} %bitcast.27), calls=%async_computation.1 | async-start | bytes 2097152 | tf_op jit(solution)/shard_map/all_to_all | solution.py:104
  91.7 59.7 %all-to-all-start.3 = ((bf16[8,128,512]{1,2,0:T(8,128)(2,1)}), bf16[8,128,512]{1,2,0:T(8,128)(2,1)}, u32[]{:S(2)}, u32[]{:S(2)}) async-start(bf16[8,128,512]{1,2,0:T(8,128)(2,1)} %bitcast.33), calls=%async_computation.3 | async-start | bytes 2097152 | tf_op jit(solution)/shard_map/all_to_all | solution.py:52
  117.6 49.6 %collective-permute-start.6 = (bf16[64,1024]{1,0:T(8,128)(2,1)S(1)}, bf16[64,1024]{1,0:T(8,128)(2,1)S(1)}, u32[]{:S(2)}, u32[]{:S(2)}) collective-permute-start(bf16[64,1024]{1,0:T(8,128)(2,1)S(1)} %select_convert_fusion.1), channel_id=1, source_target_pairs={{0,256},{256,0},{1,257},{257,1},{2,258},{258,2},{3,259},{259,3},{4... | collective-permute-start | bytes 393224 | tf_op jit(solution)/shard_map/ppermute | solution.py:18
  158.2 17.0 %collective-permute-start.7 = (bf16[400,512]{1,0:T(8,128)(2,1)}, bf16[400,512]{1,0:T(8,128)(2,1)}, u32[]{:S(2)}, u32[]{:S(2)}) collective-permute-start(bf16[400,512]{1,0:T(8,128)(2,1)} %get-tuple-element.16), channel_id=1, source_target_pairs={{0,16},{16,0},{32,48},{48,32},{1,17},{17,1},{33,49},{49,33},{2,18}... | collective-permute-start | bytes 1228808 | tf_op jit(solution)/shard_map/ppermute | solution.py:22
  160.1 22.0 %collective-permute-start.9 = (bf16[400,512]{1,0:T(8,128)(2,1)S(1)}, bf16[400,512]{1,0:T(8,128)(2,1)}, u32[]{:S(2)}, u32[]{:S(2)}) collective-permute-start(bf16[400,512]{1,0:T(8,128)(2,1)S(1)} %get-tuple-element.17), channel_id=1, source_target_pairs={{0,48},{16,32},{32,16},{48,0},{1,49},{17,33},{33,17},{49,1},{2,50}... | collective-permute-start | bytes 1228808 | tf_op jit(solution)/shard_map/ppermute | solution.py:22
  162.3 19.9 %collective-permute-start.8 = (bf16[400,512]{1,0:T(8,128)(2,1)S(1)}, bf16[400,512]{1,0:T(8,128)(2,1)}, u32[]{:S(2)}, u32[]{:S(2)}) collective-permute-start(bf16[400,512]{1,0:T(8,128)(2,1)S(1)} %get-tuple-element.18), channel_id=1, source_target_pairs={{0,32},{16,48},{32,0},{48,16},{1,33},{17,49},{33,1},{49,17},{2,34}... | collective-permute-start | bytes 1228808 | tf_op jit(solution)/shard_map/ppermute | solution.py:22
  168.0 28.9 %all-to-all-start.2 = ((bf16[8,64,128]{2,1,0:T(8,128)(2,1)}), bf16[8,64,128]{2,1,0:T(8,128)(2,1)S(1)}, u32[]{:S(2)}, u32[]{:S(2)}) async-start(bf16[8,64,128]{2,1,0:T(8,128)(2,1)} %copy.39), calls=%async_computation.2 | async-start | bytes 262144 | tf_op jit(solution)/shard_map/all_to_all | solution.py:111
  185.9 29.3 %collective-permute-start.10 = (bf16[208,512]{1,0:T(8,128)(2,1)S(1)}, bf16[208,512]{1,0:T(8,128)(2,1)S(1)}, u32[]{:S(2)}, u32[]{:S(2)}) collective-permute-start(bf16[208,512]{1,0:T(8,128)(2,1)S(1)} %pad_maximum_fusion.3), channel_id=1, source_target_pairs={{0,8},{8,0},{1,9},{9,1},{2,10},{10,2},{3,11},{11,3},{4,12},{12,4},... | collective-permute-start | bytes 638984 | tf_op jit(solution)/shard_map/ppermute | solution.py:18
where the time goes:
time: 218 us; the launch traced here: 217 us
  starting transfers between devices  109 us (50%)
  waiting for transfers between devices  68.8 us (32%)
  matrix products  11.8 us (5%)
  local copies, waits for them, and re-layouts  9.26 us (4%)
  blocking collectives  8.92 us (4%)
  other arithmetic  7.69 us (4%)
    ppermute x5, starting transfers between devices, swap(): return lax.ppermute(value, axis, [(0, 1), (1, 0)])  50.8 us
    all_to_all x1, waiting for transfers between devices, local(): ctx = lax.all_to_all(feature_rows, GROUP, 0, 0, tiled=True)  26.7 us
    all_to_all x1, starting transfers between devices, local(): ctx = lax.all_to_all(feature_rows, GROUP, 0, 0, tiled=True)  25.6 us
    ppermute x5, waiting for transfers between devices, swap(): return lax.ppermute(value, axis, [(0, 1), (1, 0)])  22.5 us
    ppermute x6, starting transfers between devices, crossed(): lax.ppermute(value, axis, [(i, i ^ k) for i in range(lax.axis_size(axis))])  18.6 us
    ppermute x6, waiting for transfers between devices, crossed(): lax.ppermute(value, axis, [(i, i ^ k) for i in range(lax.axis_size(axis))])  11.3 us
    all_gather x1, blocking collectives, local(): stats = lax.all_gather(stats, 'y')  8.92 us
    all_to_all x1, waiting for transfers between devices, local(): partial = lax.all_to_all(partial, 'y', 0, 0, tiled=True)  8.26 us
  transfers between devices with their start and end apart: 15, of which 7 were waited for; matrix products, arithmetic and copies ran while one was open for 8% of the time, Pallas kernels for 0%

commit v1 on v0

--- a/solution.py
+++ b/solution.py
@@ -44,13 +44,18 @@
     width = cols * lax.axis_size(DP)
     xs, ys = lax.axis_size("x"), lax.axis_size("y")
     members = lax.axis_size(GROUP)
-    x, zh, c, zi = (lax.axis_index(a) for a in ("x", "zh", "c", "zi"))
+    x, y, zh, c, zi = (lax.axis_index(a) for a in ("x", "y", "zh", "c", "zi"))
     blocks = feats // (members * rows)
 
-    feature_rows = context.reshape(tok, blocks, members, rows).transpose(2, 0, 1, 3)
-    feature_rows = feature_rows.reshape(members, tok, blocks * rows)
-    ctx = lax.all_to_all(feature_rows, GROUP, 0, 0, tiled=True)
-    ctx = ctx.reshape(members * tok, blocks * rows)
+    feature_rows = lax.dynamic_slice_in_dim(context, y * (feats // ys), feats // ys, 1)
+    feature_rows = feature_rows.reshape(tok, 2, members, rows).transpose(2, 0, 1, 3)
+    feature_rows = feature_rows.reshape(members, tok, 2 * rows)
+    quarter = lax.all_to_all(feature_rows, GROUP, 0, 0, tiled=True)
+    quarter = quarter.reshape(members * tok, 2 * rows)
+    ctx = jnp.zeros((members * tok, blocks * rows), BF16)
+    for k in range(ys):
+        piece = quarter if k == 0 else crossed(quarter, "y", k)
+        ctx = lax.dynamic_update_slice_in_dim(ctx, piece, (y ^ k) * 2 * rows, 1)
 
     weight = out_weight.transpose(1, 0, 2)
     other = swap(weight, "zh")
@@ -117,7 +122,8 @@
         update = lax.dot_general(
             masked, grads, (((0,), (0,)), ((), ())), preferred_element_type=F32
         )
-        updates.append(update.astype(BF16).reshape(xs, 2 * rows, cols))
+        update = update.astype(BF16)
+        updates.append(update.reshape(xs, 2 * rows, cols))
     gain_rows = jnp.pad(two_terms(gain_part), ((0, 16 - 2 * towers), (0, 0)))
     updates.append(jnp.broadcast_to(gain_rows[None], (xs, 16, cols)))
     updates = jnp.concatenate(updates, axis=1)

time: 218 us -> 204 us (0.936)
  waiting for transfers between devices: 68.8 us -> 56.8 us
  matrix products: 11.8 us -> 7.65 us
    all_to_all x1, starting transfers between devices: 25.6 us -> 6.29 us  [local(): quarter = lax.all_to_all(feature_rows, GROUP, 0, 0, tiled=True)]
    all_to_all x1, waiting for transfers between devices: 26.7 us -> 7.95 us  [local(): quarter = lax.all_to_all(feature_rows, GROUP, 0, 0, tiled=True)]
    all_to_all x1, starting transfers between devices: 7.18 us -> 24 us  [local(): settled = lax.all_to_all(total, GROUP, 0, 0, tiled=True)]
    ppermute x6 -> x9, starting transfers between devices: 18.6 us -> 27.9 us  [crossed(): lax.ppermute(value, axis, [(i, i ^ k) for i in range(lax.axis_size(axis))])]
    all_to_all x1, waiting for transfers between devices: 8.26 us -> 0.01 us  [local(): partial = lax.all_to_all(partial, 'y', 0, 0, tiled=True)]
    ppermute x5, starting transfers between devices: 50.8 us -> 43.1 us  [swap(): return lax.ppermute(value, axis, [(0, 1), (1, 0)])]
    ppermute x6 -> x9, waiting for transfers between devices: 11.3 us -> 18.5 us  [crossed(): lax.ppermute(value, axis, [(i, i ^ k) for i in range(lax.axis_size(axis))])]
    all_to_all x1, waiting for transfers between devices: 0.01 us -> 4.34 us  [local(): settled = lax.all_to_all(total, GROUP, 0, 0, tiled=True)]
  transfers between devices with their start and end apart: 15 -> 18, of which waited for: 7 -> 9; matrix products, arithmetic and copies ran while one was open for 8% -> 8% of each run, Pallas kernels for 0% -> 0%
where the time goes in v1:
time: 204 us; the launch traced here: 203 us
  starting transfers between devices  109 us (53%)
  waiting for transfers between devices  56.8 us (28%)
  local copies, waits for them, and re-layouts  10.9 us (5%)
  blocking collectives  8.79 us (4%)
  other arithmetic  8.17 us (4%)
  matrix products  7.65 us (4%)
    ppermute x5, starting transfers between devices, swap(): return lax.ppermute(value, axis, [(0, 1), (1, 0)])  43.1 us
    ppermute x9, starting transfers between devices, crossed(): lax.ppermute(value, axis, [(i, i ^ k) for i in range(lax.axis_size(axis))])  27.9 us
    ppermute x5, waiting for transfers between devices, swap(): return lax.ppermute(value, axis, [(0, 1), (1, 0)])  26 us
    all_to_all x1, starting transfers between devices, local(): settled = lax.all_to_all(total, GROUP, 0, 0, tiled=True)  24 us
    ppermute x9, waiting for transfers between devices, crossed(): lax.ppermute(value, axis, [(i, i ^ k) for i in range(lax.axis_size(axis))])  18.5 us
    all_gather x1, blocking collectives, local(): stats = lax.all_gather(stats, 'y')  8.79 us
    all_to_all x1, waiting for transfers between devices, local(): quarter = lax.all_to_all(feature_rows, GROUP, 0, 0, tiled=True)  7.95 us
    all_to_all x1, starting transfers between devices, local(): quarter = lax.all_to_all(feature_rows, GROUP, 0, 0, tiled=True)  6.29 us
  transfers between devices with their start and end apart: 18, of which 9 were waited for; matrix products, arithmetic and copies ran while one was open for 8% of the time, Pallas kernels for 0%

profile of v1, /device:TPU:1, one launch (start us, length us, event | category | flops | bytes accessed | tf_op | source)
XLA Modules:
  0.0 202.7 jit_solution(848231568201323917)
XLA Ops:
  0.7 1.5 fusion.16
  2.2 8.8 %all-gather.1 = f32[4,2,128]{2,1,0:T(2,128)S(1)} all-gather(f32[1,2,128]{2,1,0:T(2,128)S(1)} %maximum_bitcast_fusion), channel_id=2, replica_groups=mesh['zi'=2,'y'=4,'x'=4,'zh'=2,'zl'=4,'c'=2] {'y'}, dimensions={0}, use_global_device_ids=true | all-gather | bytes 5120 | tf_op jit(solution)/shard_map/all_gather | solution.py:80
  11.0 15.4 %collective-permute-start = (f32[2,128]{1,0:T(2,128)S(1)}, f32[2,128]{1,0:T(2,128)S(1)}, u32[]{:S(2)}, u32[]{:S(2)}) collective-permute-start(f32[2,128]{1,0:T(2,128)S(1)} %reduce_sum.47), channel_id=1, source_target_pairs={{0,256},{256,0},{1,257},{257,1},{2,258},{258,2},{3,259},{259,3},{4... | collective-permute-start | bytes 3080 | tf_op jit(solution)/shard_map/ppermute | solution.py:18
  26.7 0.7 copy.41
  27.4 6.3 %all-to-all-start.3 = ((bf16[8,128,128]{1,2,0:T(8,128)(2,1)}), bf16[8,128,128]{1,2,0:T(8,128)(2,1)S(1)}, u32[]{:S(2)}, u32[]{:S(2)}) async-start(bf16[8,128,128]{1,2,0:T(8,128)(2,1)} %bitcast.30), calls=%async_computation.3 | async-start | bytes 524288 | tf_op jit(solution)/shard_map/all_to_all | solution.py:53
  34.4 8.0 %all-to-all-done.3 = bf16[8,128,128]{1,2,0:T(8,128)(2,1)S(1)} async-done(((bf16[8,128,128]{1,2,0:T(8,128)(2,1)}), bf16[8,128,128]{1,2,0:T(8,128)(2,1)S(1)}, u32[]{:S(2)}, u32[]{:S(2)}) %all-to-all-start.3) | async-done | bytes 262176 | tf_op jit(solution)/shard_map/all_to_all | solution.py:53
  42.4 0.9 broadcast_in_dim.62
  43.3 3.5 %all-to-all-start = ((bf16[4,144,512]{2,1,0:T(8,128)(2,1)}), bf16[4,144,512]{2,1,0:T(8,128)(2,1)S(1)}, u32[]{:S(2)}, u32[]{:S(2)}) async-start(bf16[4,144,512]{2,1,0:T(8,128)(2,1)} %broadcast_in_dim.62), calls=%async_computation | async-start | bytes 1179648 | tf_op jit(solution)/shard_map/all_to_all | solution.py:96
  46.8 4.0 %collective-permute-start.2 = (bf16[3,64,512]{2,1,0:T(8,128)(2,1)S(1)}, bf16[3,64,512]{2,1,0:T(8,128)(2,1)S(1)}, u32[]{:S(2)}, u32[]{:S(2)}) collective-permute-start(bf16[3,64,512]{2,1,0:T(8,128)(2,1)S(1)} %bitcast.142), channel_id=1, source_target_pairs={{0,8},{8,0},{1,9},{9,1},{2,10},{10,2},{3,11},{11,3},{4,12},{12,4},... | collective-permute-start | bytes 589832 | tf_op jit(solution)/shard_map/ppermute | solution.py:18
  50.8 9.2 %collective-permute-done.2 = bf16[3,64,512]{2,1,0:T(8,128)(2,1)S(1)} collective-permute-done((bf16[3,64,512]{2,1,0:T(8,128)(2,1)S(1)}, bf16[3,64,512]{2,1,0:T(8,128)(2,1)S(1)}, u32[]{:S(2)}, u32[]{:S(2)}) %collective-permute-start.2) | collective-permute-done | bytes 196640 | tf_op jit(solution)/shard_map/ppermute | solution.py:18
  60.7 0.8 pad_maximum_fusion.2
  61.5 3.1 %collective-permute-start.3 = (bf16[3,2,64,512]{3,2,1,0:T(8,128)(2,1)}, bf16[3,2,64,512]{3,2,1,0:T(8,128)(2,1)}, u32[]{:S(2)}, u32[]{:S(2)}) collective-permute-start(bf16[3,2,64,512]{3,2,1,0:T(8,128)(2,1)} %pad_maximum_fusion.2), channel_id=1, source_target_pairs={{0,16},{16,0},{32,48},{48,32},{1,17},{17,1},{33,49},{49,33},{2,18}... | collective-permute-start | bytes 1179656 | tf_op jit(solution)/shard_map/ppermute | solution.py:22
  64.6 4.4 %collective-permute-start.4 = (bf16[3,2,64,512]{3,2,1,0:T(8,128)(2,1)}, bf16[3,2,64,512]{3,2,1,0:T(8,128)(2,1)}, u32[]{:S(2)}, u32[]{:S(2)}) collective-permute-start(bf16[3,2,64,512]{3,2,1,0:T(8,128)(2,1)} %pad_maximum_fusion.2), channel_id=1, source_target_pairs={{0,32},{16,48},{32,0},{48,16},{1,33},{17,49},{33,1},{49,17},{2,34}... | collective-permute-start | bytes 1179656 | tf_op jit(solution)/shard_map/ppermute | solution.py:22
  69.0 2.2 %collective-permute-start.5 = (bf16[3,2,64,512]{3,2,1,0:T(8,128)(2,1)}, bf16[3,2,64,512]{3,2,1,0:T(8,128)(2,1)S(1)}, u32[]{:S(2)}, u32[]{:S(2)}) collective-permute-start(bf16[3,2,64,512]{3,2,1,0:T(8,128)(2,1)} %pad_maximum_fusion.2), channel_id=1, source_target_pairs={{0,48},{16,32},{32,16},{48,0},{1,49},{17,33},{33,17},{49,1},{2,50}... | collective-permute-start | bytes 1179656 | tf_op jit(solution)/shard_map/ppermute | solution.py:22
  71.5 1.0 bitcast_dynamic-update-slice_fusion.1
  72.6 4.3 %collective-permute-done.4 = bf16[3,2,64,512]{3,2,1,0:T(8,128)(2,1)} collective-permute-done((bf16[3,2,64,512]{3,2,1,0:T(8,128)(2,1)}, bf16[3,2,64,512]{3,2,1,0:T(8,128)(2,1)}, u32[]{:S(2)}, u32[]{:S(2)}) %collective-permute-start.4) | collective-permute-done | bytes 393248 | tf_op jit(solution)/shard_map/ppermute | solution.py:22
  76.8 1.0 bitcast_dynamic-update-slice_fusion
  77.8 3.0 %collective-permute-done.5 = bf16[3,2,64,512]{3,2,1,0:T(8,128)(2,1)S(1)} collective-permute-done((bf16[3,2,64,512]{3,2,1,0:T(8,128)(2,1)}, bf16[3,2,64,512]{3,2,1,0:T(8,128)(2,1)S(1)}, u32[]{:S(2)}, u32[]{:S(2)}) %collective-permute-start.5) | collective-permute-done | bytes 393248 | tf_op jit(solution)/shard_map/ppermute | solution.py:22
  80.9 1.1 copy.42
  82.0 2.5 %collective-permute-start.8 = (bf16[1024,128]{1,0:T(8,128)(2,1)S(1)}, bf16[1024,128]{1,0:T(8,128)(2,1)}, u32[]{:S(2)}, u32[]{:S(2)}) collective-permute-start(bf16[1024,128]{1,0:T(8,128)(2,1)S(1)} %bitcast.130), channel_id=1, source_target_pairs={{0,128},{64,192},{128,0},{192,64},{1,129},{65,193},{129,1},{193,65... | collective-permute-start | bytes 786440 | tf_op jit(solution)/shard_map/ppermute | solution.py:22
  84.5 1.9 collective-permute-start.7
  86.4 11.7 %collective-permute-start.1 = (bf16[4,144,512]{2,1,0:T(8,128)(2,1)S(1)}, bf16[4,144,512]{2,1,0:T(8,128)(2,1)S(1)}, u32[]{:S(2)}, u32[]{:S(2)}) collective-permute-start(bf16[4,144,512]{2,1,0:T(8,128)(2,1)S(1)} %all-to-all-done), channel_id=1, source_target_pairs={{0,1},{1,0},{2,3},{3,2},{4,5},{5,4},{6,7},{7,6},{8,9},{9,8},{10,11... | collective-permute-start | bytes 1769480 | tf_op jit(solution)/shard_map/ppermute | solution.py:18
  98.3 4.9 %collective-permute-start.9 = (bf16[1024,128]{1,0:T(8,128)(2,1)S(1)}, bf16[1024,128]{1,0:T(8,128)(2,1)S(1)}, u32[]{:S(2)}, u32[]{:S(2)}) collective-permute-start(bf16[1024,128]{1,0:T(8,128)(2,1)S(1)} %bitcast.132), channel_id=1, source_target_pairs={{0,192},{64,128},{128,64},{192,0},{1,193},{65,129},{129,65},{193,1... | collective-permute-start | bytes 786440 | tf_op jit(solution)/shard_map/ppermute | solution.py:22
  103.3 1.0 constant_dynamic-update-slice_fusion.2
  104.3 1.0 constant_dynamic-update-slice_fusion.1
  105.3 4.4 %collective-permute-done.9 = bf16[1024,128]{1,0:T(8,128)(2,1)S(1)} collective-permute-done((bf16[1024,128]{1,0:T(8,128)(2,1)S(1)}, bf16[1024,128]{1,0:T(8,128)(2,1)S(1)}, u32[]{:S(2)}, u32[]{:S(2)}) %collective-permute-start.9) | collective-permute-done | bytes 262176 | tf_op jit(solution)/shard_map/ppermute | solution.py:22
  110.3 0.8 convolution_convert_fusion
  111.1 0.8 convolution_convert_fusion.1
  112.0 0.8 convolution_convert_fusion.2
  113.0 0.8 dynamic-slice_bitcast_fusion.2
  113.9 1.9 collective-permute-start.10
  115.8 3.1 %collective-permute-start.12 = (bf16[400,512]{1,0:T(8,128)(2,1)S(1)}, bf16[400,512]{1,0:T(8,128)(2,1)}, u32[]{:S(2)}, u32[]{:S(2)}) collective-permute-start(bf16[400,512]{1,0:T(8,128)(2,1)S(1)} %get-tuple-element.20), channel_id=1, source_target_pairs={{0,48},{16,32},{32,16},{48,0},{1,49},{17,33},{33,17},{49,1},{2,50}... | collective-permute-start | bytes 1228808 | tf_op jit(solution)/shard_map/ppermute | solution.py:22
  118.9 3.9 %collective-permute-start.11 = (bf16[400,512]{1,0:T(8,128)(2,1)S(1)}, bf16[400,512]{1,0:T(8,128)(2,1)}, u32[]{:S(2)}, u32[]{:S(2)}) collective-permute-start(bf16[400,512]{1,0:T(8,128)(2,1)S(1)} %get-tuple-element.21), channel_id=1, source_target_pairs={{0,32},{16,48},{32,0},{48,16},{1,33},{17,49},{33,1},{49,17},{2,34}... | collective-permute-start | bytes 1228808 | tf_op jit(solution)/shard_map/ppermute | solution.py:22
  122.9 0.7 fusion.45
  123.6 0.7 fusion.44
  124.4 1.8 add_convert_fusion
  126.2 4.2 %all-to-all-start.1 = ((bf16[4,128,1024]{2,1,0:T(8,128)(2,1)}), bf16[4,128,1024]{2,1,0:T(8,128)(2,1)}, u32[]{:S(2)}, u32[]{:S(2)}) async-start(bf16[4,128,1024]{2,1,0:T(8,128)(2,1)} %bitcast.126), calls=%async_computation.1 | async-start | bytes 2097152 | tf_op jit(solution)/shard_map/all_to_all | solution.py:109
  131.2 6.8 %collective-permute-done.12 = bf16[400,512]{1,0:T(8,128)(2,1)} collective-permute-done((bf16[400,512]{1,0:T(8,128)(2,1)S(1)}, bf16[400,512]{1,0:T(8,128)(2,1)}, u32[]{:S(2)}, u32[]{:S(2)}) %collective-permute-start.12) | collective-permute-done | bytes 409632 | tf_op jit(solution)/shard_map/ppermute | solution.py:22
  139.5 1.4 fusion.6
  141.0 10.1 %collective-permute-start.13 = (bf16[208,512]{1,0:T(8,128)(2,1)S(1)}, bf16[208,512]{1,0:T(8,128)(2,1)S(1)}, u32[]{:S(2)}, u32[]{:S(2)}) collective-permute-start(bf16[208,512]{1,0:T(8,128)(2,1)S(1)} %pad_maximum_fusion.3), channel_id=1, source_target_pairs={{0,8},{8,0},{1,9},{9,1},{2,10},{10,2},{3,11},{11,3},{4,12},{12,4},... | collective-permute-start | bytes 638984 | tf_op jit(solution)/shard_map/ppermute | solution.py:18
  151.1 4.2 %collective-permute-done.13 = bf16[208,512]{1,0:T(8,128)(2,1)S(1)} collective-permute-done((bf16[208,512]{1,0:T(8,128)(2,1)S(1)}, bf16[208,512]{1,0:T(8,128)(2,1)S(1)}, u32[]{:S(2)}, u32[]{:S(2)}) %collective-permute-start.13) | collective-permute-done | bytes 213024 | tf_op jit(solution)/shard_map/ppermute | solution.py:18
  155.3 1.5 convert_reduce_fusion
  156.8 1.9 collective-permute-start.6
  158.7 12.7 %collective-permute-done.6 = bf16[64,1024]{1,0:T(8,128)(2,1)S(1)} collective-permute-done((bf16[64,1024]{1,0:T(8,128)(2,1)S(1)}, bf16[64,1024]{1,0:T(8,128)(2,1)S(1)}, u32[]{:S(2)}, u32[]{:S(2)}) %collective-permute-start.6) | collective-permute-done | bytes 131104 | tf_op jit(solution)/shard_map/ppermute | solution.py:18
  172.2 24.0 %all-to-all-start.2 = ((bf16[8,64,128]{2,1,0:T(8,128)(2,1)}), bf16[8,64,128]{2,1,0:T(8,128)(2,1)S(1)}, u32[]{:S(2)}, u32[]{:S(2)}) async-start(bf16[8,64,128]{2,1,0:T(8,128)(2,1)} %copy.39), calls=%async_computation.2 | async-start | bytes 262144 | tf_op jit(solution)/shard_map/all_to_all | solution.py:116
  196.8 0.8 fusion.10
  197.6 4.3 %all-to-all-done.2 = bf16[8,64,128]{2,1,0:T(8,128)(2,1)S(1)} async-done(((bf16[8,64,128]{2,1,0:T(8,128)(2,1)}), bf16[8,64,128]{2,1,0:T(8,128)(2,1)S(1)}, u32[]{:S(2)}, u32[]{:S(2)}) %all-to-all-start.2) | async-done | bytes 131104 | tf_op jit(solution)/shard_map/all_to_all | solution.py:116
  202.0 0.8 copy.45
  (75 shorter events, 6.4 us)
Async XLA Ops:
  0.6 25.8 %copy-start = (bf16[128,4096]{1,0:T(8,128)(2,1)S(1)}, bf16[128,4096]{1,0:T(8,128)(2,1)}, u32[]{:S(2)}) copy-start(bf16[128,4096]{1,0:T(8,128)(2,1)} %param.6) | copy-start | bytes 3145732
  0.6 33.0 %copy-start.7 = (s32[128]{0:T(128)S(1)}, s32[128]{0:T(128)}, u32[]{:S(2)}) copy-start(s32[128]{0:T(128)} %param.9) | copy-start | bytes 1540
  0.7 33.1 %copy-start.4 = (bf16[128,512]{1,0:T(8,128)(2,1)S(1)}, bf16[128,512]{1,0:T(8,128)(2,1)}, u32[]{:S(2)}) copy-start(bf16[128,512]{1,0:T(8,128)(2,1)} %param.7) | copy-start | bytes 393220
  0.7 33.1 %copy-start.6 = (bf16[128,512]{1,0:T(8,128)(2,1)S(1)}, bf16[128,512]{1,0:T(8,128)(2,1)}, u32[]{:S(2)}) copy-start(bf16[128,512]{1,0:T(8,128)(2,1)} %param.8) | copy-start | bytes 393220
  11.0 22.7 %collective-permute-start = (f32[2,128]{1,0:T(2,128)S(1)}, f32[2,128]{1,0:T(2,128)S(1)}, u32[]{:S(2)}, u32[]{:S(2)}) collective-permute-start(f32[2,128]{1,0:T(2,128)S(1)} %reduce_sum.47), channel_id=1, source_target_pairs={{0,256},{256,0},{1,257},{257,1},{2,258},{258,2},{3,259},{259,3},{4... | collective-permute-start | bytes 3080 | tf_op jit(solution)/shard_map/ppermute | solution.py:18
  27.4 15.0 %all-to-all-start.3 = ((bf16[8,128,128]{1,2,0:T(8,128)(2,1)}), bf16[8,128,128]{1,2,0:T(8,128)(2,1)S(1)}, u32[]{:S(2)}, u32[]{:S(2)}) async-start(bf16[8,128,128]{1,2,0:T(8,128)(2,1)} %bitcast.30), calls=%async_computation.3 | async-start | bytes 524288 | tf_op jit(solution)/shard_map/all_to_all | solution.py:53
  33.7 13.1 %copy-start.5 = (bf16[64,3,512]{2,0,1:T(8,128)(2,1)S(1)}, bf16[64,3,512]{2,0,1:T(8,128)(2,1)}, u32[]{:S(2)}) copy-start(bf16[64,3,512]{2,0,1:T(8,128)(2,1)} %param.10) | copy-start | bytes 589828
  42.4 26.6 %copy-start.3 = (bf16[8,128,128]{1,2,0:T(8,128)(2,1)}, bf16[8,128,128]{1,2,0:T(8,128)(2,1)S(1)}, u32[]{:S(2)}) copy-start(bf16[8,128,128]{1,2,0:T(8,128)(2,1)S(1)} %all-to-all-done.3) | copy-start | bytes 786436
  43.3 43.1 %all-to-all-start = ((bf16[4,144,512]{2,1,0:T(8,128)(2,1)}), bf16[4,144,512]{2,1,0:T(8,128)(2,1)S(1)}, u32[]{:S(2)}, u32[]{:S(2)}) async-start(bf16[4,144,512]{2,1,0:T(8,128)(2,1)} %broadcast_in_dim.62), calls=%async_computation | async-start | bytes 1179648 | tf_op jit(solution)/shard_map/all_to_all | solution.py:96
  46.8 13.2 %collective-permute-start.2 = (bf16[3,64,512]{2,1,0:T(8,128)(2,1)S(1)}, bf16[3,64,512]{2,1,0:T(8,128)(2,1)S(1)}, u32[]{:S(2)}, u32[]{:S(2)}) collective-permute-start(bf16[3,64,512]{2,1,0:T(8,128)(2,1)S(1)} %bitcast.142), channel_id=1, source_target_pairs={{0,8},{8,0},{1,9},{9,1},{2,10},{10,2},{3,11},{11,3},{4,12},{12,4},... | collective-permute-start | bytes 589832 | tf_op jit(solution)/shard_map/ppermute | solution.py:18
  60.0 0.7 copy-start.1
  61.5 10.0 %collective-permute-start.3 = (bf16[3,2,64,512]{3,2,1,0:T(8,128)(2,1)}, bf16[3,2,64,512]{3,2,1,0:T(8,128)(2,1)}, u32[]{:S(2)}, u32[]{:S(2)}) collective-permute-start(bf16[3,2,64,512]{3,2,1,0:T(8,128)(2,1)} %pad_maximum_fusion.2), channel_id=1, source_target_pairs={{0,16},{16,0},{32,48},{48,32},{1,17},{17,1},{33,49},{49,33},{2,18}... | collective-permute-start | bytes 1179656 | tf_op jit(solution)/shard_map/ppermute | solution.py:22
  64.6 12.2 %collective-permute-start.4 = (bf16[3,2,64,512]{3,2,1,0:T(8,128)(2,1)}, bf16[3,2,64,512]{3,2,1,0:T(8,128)(2,1)}, u32[]{:S(2)}, u32[]{:S(2)}) collective-permute-start(bf16[3,2,64,512]{3,2,1,0:T(8,128)(2,1)} %pad_maximum_fusion.2), channel_id=1, source_target_pairs={{0,32},{16,48},{32,0},{48,16},{1,33},{17,49},{33,1},{49,17},{2,34}... | collective-permute-start | bytes 1179656 | tf_op jit(solution)/shard_map/ppermute | solution.py:22
  69.0 2.4 %copy-start.2 = (bf16[3,1,64,512]{3,2,1,0:T(8,128)(2,1)S(1)}, bf16[3,1,64,512]{3,2,1,0:T(8,128)(2,1)}, u32[]{:S(2)}) copy-start(bf16[3,1,64,512]{3,2,1,0:T(8,128)(2,1)} %copy-done.1) | copy-start | bytes 589828
  69.0 11.8 %collective-permute-start.5 = (bf16[3,2,64,512]{3,2,1,0:T(8,128)(2,1)}, bf16[3,2,64,512]{3,2,1,0:T(8,128)(2,1)S(1)}, u32[]{:S(2)}, u32[]{:S(2)}) collective-permute-start(bf16[3,2,64,512]{3,2,1,0:T(8,128)(2,1)} %pad_maximum_fusion.2), channel_id=1, source_target_pairs={{0,48},{16,32},{32,16},{48,0},{1,49},{17,33},{33,17},{49,1},{2,50}... | collective-permute-start | bytes 1179656 | tf_op jit(solution)/shard_map/ppermute | solution.py:22
  82.0 22.3 %collective-permute-start.8 = (bf16[1024,128]{1,0:T(8,128)(2,1)S(1)}, bf16[1024,128]{1,0:T(8,128)(2,1)}, u32[]{:S(2)}, u32[]{:S(2)}) collective-permute-start(bf16[1024,128]{1,0:T(8,128)(2,1)S(1)} %bitcast.130), channel_id=1, source_target_pairs={{0,128},{64,192},{128,0},{192,64},{1,129},{65,193},{129,1},{193,65... | collective-permute-start | bytes 786440 | tf_op jit(solution)/shard_map/ppermute | solution.py:22
  84.5 18.8 %collective-permute-start.7 = (bf16[1024,128]{1,0:T(8,128)(2,1)S(1)}, bf16[1024,128]{1,0:T(8,128)(2,1)}, u32[]{:S(2)}, u32[]{:S(2)}) collective-permute-start(bf16[1024,128]{1,0:T(8,128)(2,1)S(1)} %bitcast.131), channel_id=1, source_target_pairs={{0,64},{64,0},{128,192},{192,128},{1,65},{65,1},{129,193},{193,129... | collective-permute-start | bytes 786440 | tf_op jit(solution)/shard_map/ppermute | solution.py:22
  86.4 23.4 %collective-permute-start.1 = (bf16[4,144,512]{2,1,0:T(8,128)(2,1)S(1)}, bf16[4,144,512]{2,1,0:T(8,128)(2,1)S(1)}, u32[]{:S(2)}, u32[]{:S(2)}) collective-permute-start(bf16[4,144,512]{2,1,0:T(8,128)(2,1)S(1)} %all-to-all-done), channel_id=1, source_target_pairs={{0,1},{1,0},{2,3},{3,2},{4,5},{5,4},{6,7},{7,6},{8,9},{9,8},{10,11... | collective-permute-start | bytes 1769480 | tf_op jit(solution)/shard_map/ppermute | solution.py:18
  98.3 11.5 %collective-permute-start.9 = (bf16[1024,128]{1,0:T(8,128)(2,1)S(1)}, bf16[1024,128]{1,0:T(8,128)(2,1)S(1)}, u32[]{:S(2)}, u32[]{:S(2)}) collective-permute-start(bf16[1024,128]{1,0:T(8,128)(2,1)S(1)} %bitcast.132), channel_id=1, source_target_pairs={{0,192},{64,128},{128,64},{192,0},{1,193},{65,129},{129,65},{193,1... | collective-permute-start | bytes 786440 | tf_op jit(solution)/shard_map/ppermute | solution.py:22
  113.9 16.6 %collective-permute-start.10 = (bf16[400,512]{1,0:T(8,128)(2,1)}, bf16[400,512]{1,0:T(8,128)(2,1)}, u32[]{:S(2)}, u32[]{:S(2)}) collective-permute-start(bf16[400,512]{1,0:T(8,128)(2,1)} %get-tuple-element.19), channel_id=1, source_target_pairs={{0,16},{16,0},{32,48},{48,32},{1,17},{17,1},{33,49},{49,33},{2,18}... | collective-permute-start | bytes 1228808 | tf_op jit(solution)/shard_map/ppermute | solution.py:22
  115.8 22.2 %collective-permute-start.12 = (bf16[400,512]{1,0:T(8,128)(2,1)S(1)}, bf16[400,512]{1,0:T(8,128)(2,1)}, u32[]{:S(2)}, u32[]{:S(2)}) collective-permute-start(bf16[400,512]{1,0:T(8,128)(2,1)S(1)} %get-tuple-element.20), channel_id=1, source_target_pairs={{0,48},{16,32},{32,16},{48,0},{1,49},{17,33},{33,17},{49,1},{2,50}... | collective-permute-start | bytes 1228808 | tf_op jit(solution)/shard_map/ppermute | solution.py:22
  118.9 19.8 %collective-permute-start.11 = (bf16[400,512]{1,0:T(8,128)(2,1)S(1)}, bf16[400,512]{1,0:T(8,128)(2,1)}, u32[]{:S(2)}, u32[]{:S(2)}) collective-permute-start(bf16[400,512]{1,0:T(8,128)(2,1)S(1)} %get-tuple-element.21), channel_id=1, source_target_pairs={{0,32},{16,48},{32,0},{48,16},{1,33},{17,49},{33,1},{49,17},{2,34}... | collective-permute-start | bytes 1228808 | tf_op jit(solution)/shard_map/ppermute | solution.py:22
  126.2 29.1 %all-to-all-start.1 = ((bf16[4,128,1024]{2,1,0:T(8,128)(2,1)}), bf16[4,128,1024]{2,1,0:T(8,128)(2,1)}, u32[]{:S(2)}, u32[]{:S(2)}) async-start(bf16[4,128,1024]{2,1,0:T(8,128)(2,1)} %bitcast.126), calls=%async_computation.1 | async-start | bytes 2097152 | tf_op jit(solution)/shard_map/all_to_all | solution.py:109
  141.0 14.3 %collective-permute-start.13 = (bf16[208,512]{1,0:T(8,128)(2,1)S(1)}, bf16[208,512]{1,0:T(8,128)(2,1)S(1)}, u32[]{:S(2)}, u32[]{:S(2)}) collective-permute-start(bf16[208,512]{1,0:T(8,128)(2,1)S(1)} %pad_maximum_fusion.3), channel_id=1, source_target_pairs={{0,8},{8,0},{1,9},{9,1},{2,10},{10,2},{3,11},{11,3},{4,12},{12,4},... | collective-permute-start | bytes 638984 | tf_op jit(solution)/shard_map/ppermute | solution.py:18
  156.8 14.6 %collective-permute-start.6 = (bf16[64,1024]{1,0:T(8,128)(2,1)S(1)}, bf16[64,1024]{1,0:T(8,128)(2,1)S(1)}, u32[]{:S(2)}, u32[]{:S(2)}) collective-permute-start(bf16[64,1024]{1,0:T(8,128)(2,1)S(1)} %select_convert_fusion.1), channel_id=1, source_target_pairs={{0,256},{256,0},{1,257},{257,1},{2,258},{258,2},{3,259},{259,3},{4... | collective-permute-start | bytes 393224 | tf_op jit(solution)/shard_map/ppermute | solution.py:18
  172.2 29.8 %all-to-all-start.2 = ((bf16[8,64,128]{2,1,0:T(8,128)(2,1)}), bf16[8,64,128]{2,1,0:T(8,128)(2,1)S(1)}, u32[]{:S(2)}, u32[]{:S(2)}) async-start(bf16[8,64,128]{2,1,0:T(8,128)(2,1)} %copy.39), calls=%async_computation.2 | async-start | bytes 262144 | tf_op jit(solution)/shard_map/all_to_all | solution.py:116

commit v2 on v0

--- a/solution.py
+++ b/solution.py
@@ -44,13 +44,18 @@
     width = cols * lax.axis_size(DP)
     xs, ys = lax.axis_size("x"), lax.axis_size("y")
     members = lax.axis_size(GROUP)
-    x, zh, c, zi = (lax.axis_index(a) for a in ("x", "zh", "c", "zi"))
+    x, y, zh, zl, c, zi = (lax.axis_index(a) for a in ("x", "y", "zh", "zl", "c", "zi"))
     blocks = feats // (members * rows)
 
-    feature_rows = context.reshape(tok, blocks, members, rows).transpose(2, 0, 1, 3)
-    feature_rows = feature_rows.reshape(members, tok, blocks * rows)
-    ctx = lax.all_to_all(feature_rows, GROUP, 0, 0, tiled=True)
-    ctx = ctx.reshape(members * tok, blocks * rows)
+    feature_rows = lax.dynamic_slice_in_dim(context, (y & 1) * (feats // 2), feats // 2, 1)
+    feature_rows = feature_rows.reshape(tok, xs, members, rows).transpose(2, 0, 1, 3)
+    feature_rows = feature_rows.reshape(members, tok, xs * rows)
+    half = lax.all_to_all(feature_rows, GROUP, 0, 0, tiled=True)
+    half = half.reshape(members * tok, xs * rows)
+    other = crossed(half, "y", 1)
+    first = jnp.where((y & 1) == 0, half, other)
+    second = jnp.where((y & 1) == 0, other, half)
+    ctx = jnp.concatenate([first, second], axis=1)
 
     weight = out_weight.transpose(1, 0, 2)
     other = swap(weight, "zh")
@@ -74,7 +79,8 @@
     )
     stats = lax.all_gather(stats, "y")
     stats = jnp.sum(stats, axis=0)
-    stats = stats + swap(stats, "zi")
+    others = swap(stats, "zi")
+    stats = stats + others
     inverse_rms = lax.rsqrt(stats[0] / width + EPS)[:, None]
     inner = inverse_rms * stats[1][:, None]
     normed = proj_float * inverse_rms
@@ -87,9 +93,12 @@
         [grad_proj, two_terms(gain_terms), mod_row, jnp.zeros((spare, cols), BF16)], axis=0
     )
     line = lax.axis_size("zl")
-    packets = jnp.broadcast_to(packet[None], (line, *packet.shape))
-    packets = lax.all_to_all(packets, "zl", 0, 0, tiled=True)
-    packets = in_order(c, packets, swap(packets, "c"), 1).reshape(members, tok + 16, cols)
+    near = jnp.zeros((line, *packet.shape), BF16)
+    for k in range(line):
+        piece = packet if k == 0 else crossed(packet, "zl", k)
+        near = lax.dynamic_update_index_in_dim(near, piece, zl ^ k, 0)
+    others = swap(near, "c")
+    packets = in_order(c, near, others, 1).reshape(members, tok + 16, cols)
     grads = packets[:, :tok].reshape(members * tok, cols)
     gain_part = jnp.sum(joined_terms(packets[:, tok:], towers), axis=0)
     ids = packets[:, tok + 2 * towers, :tok].astype(jnp.int32).reshape(members * tok)
@@ -117,7 +126,8 @@
         update = lax.dot_general(
             masked, grads, (((0,), (0,)), ((), ())), preferred_element_type=F32
         )
-        updates.append(update.astype(BF16).reshape(xs, 2 * rows, cols))
+        update = update.astype(BF16)
+        updates.append(update.reshape(xs, 2 * rows, cols))
     gain_rows = jnp.pad(two_terms(gain_part), ((0, 16 - 2 * towers), (0, 0)))
     updates.append(jnp.broadcast_to(gain_rows[None], (xs, 16, cols)))
     updates = jnp.concatenate(updates, axis=1)
@@ -126,11 +136,10 @@
         part = lax.dynamic_index_in_dim(updates, x ^ k, 0, keepdims=False)
         parts.append(part if k == 0 else crossed(part, "x", k))
     size = towers * 2 * rows
-    weight_part = [part[:size].astype(F32) for part in parts]
-    weight_part = (weight_part[0] + weight_part[1]) + (weight_part[2] + weight_part[3])
-    weight_part = weight_part.reshape(towers, 2, rows, cols)
-    gain_part = [joined_terms(part[size:], towers) for part in parts]
-    gain_part = (gain_part[0] + gain_part[1]) + (gain_part[2] + gain_part[3])
+    parts = [part.astype(F32) for part in parts]
+    total_part = (parts[0] + parts[1]) + (parts[2] + parts[3])
+    weight_part = total_part[:size].reshape(towers, 2, rows, cols)
+    gain_part = joined_terms(total_part[size:], towers)
     kept = jnp.where(zh == 0, weight_part[:, 0], weight_part[:, 1])
     sent = jnp.where(zh == 0, weight_part[:, 1], weight_part[:, 0]).astype(BF16)
     gain_rows = jnp.pad(two_terms(gain_part), ((0, 16 - 2 * towers), (0, 0)))

time: 218 us -> 196 us (0.90)
  starting transfers between devices: 109 us -> 86 us
  waiting for transfers between devices: 68.8 us -> 79.6 us
  matrix products: 11.8 us -> 7.55 us
  local copies, waits for them, and re-layouts: 9.26 us -> 5.83 us
    all_to_all x2 -> x1, waiting for transfers between devices: 26.7 us -> 0.01 us  [local(): half = lax.all_to_all(feature_rows, GROUP, 0, 0, tiled=True)]
    ppermute x6 -> x10, waiting for transfers between devices: 11.3 us -> 34.5 us  [crossed(): lax.ppermute(value, axis, [(i, i ^ k) for i in range(lax.axis_size(axis))])]
    all_to_all x2 -> x1, starting transfers between devices: 29.1 us -> 7.28 us  [local(): half = lax.all_to_all(feature_rows, GROUP, 0, 0, tiled=True)]
    ppermute x5, starting transfers between devices: 50.8 us -> 34.2 us  [swap(): return lax.ppermute(value, axis, [(0, 1), (1, 0)])]
    ppermute x6 -> x10, starting transfers between devices: 18.6 us -> 32.1 us  [crossed(): lax.ppermute(value, axis, [(i, i ^ k) for i in range(lax.axis_size(axis))])]
    ppermute x5, waiting for transfers between devices: 22.5 us -> 35 us  [swap(): return lax.ppermute(value, axis, [(0, 1), (1, 0)])]
    dot_general x3, matrix products: 5.79 us -> 2.53 us  [local(): lax.dot_general(masked, grads, (((0,), (0,)), ((), ())), preferred_elemen...]
  transfers between devices with their start and end apart: 15 -> 18, of which waited for: 7 -> 8; matrix products, arithmetic and copies ran while one was open for 8% -> 7% of each run, Pallas kernels for 0% -> 0%
where the time goes in v2:
time: 196 us; the launch traced here: 195 us
  starting transfers between devices  86 us (44%)
  waiting for transfers between devices  79.6 us (41%)
  blocking collectives  8.27 us (4%)
  matrix products  7.55 us (4%)
  other arithmetic  6.39 us (3%)
  local copies, waits for them, and re-layouts  5.83 us (3%)
    ppermute x5, waiting for transfers between devices, swap(): return lax.ppermute(value, axis, [(0, 1), (1, 0)])  35 us
    ppermute x10, waiting for transfers between devices, crossed(): lax.ppermute(value, axis, [(i, i ^ k) for i in range(lax.axis_size(axis))])  34.5 us
    ppermute x5, starting transfers between devices, swap(): return lax.ppermute(value, axis, [(0, 1), (1, 0)])  34.2 us
    ppermute x10, starting transfers between devices, crossed(): lax.ppermute(value, axis, [(i, i ^ k) for i in range(lax.axis_size(axis))])  32.1 us
    all_to_all x1, waiting for transfers between devices, local(): partial = lax.all_to_all(partial, 'y', 0, 0, tiled=True)  10.1 us
    all_gather x1, blocking collectives, local(): stats = lax.all_gather(stats, 'y')  8.27 us
    all_to_all x1, starting transfers between devices, local(): settled = lax.all_to_all(total, GROUP, 0, 0, tiled=True)  8.2 us
    all_to_all x1, starting transfers between devices, local(): half = lax.all_to_all(feature_rows, GROUP, 0, 0, tiled=True)  7.28 us
  transfers between devices with their start and end apart: 18, of which 8 were waited for; matrix products, arithmetic and copies ran while one was open for 7% of the time, Pallas kernels for 0%

profile of v2, /device:TPU:1, one launch (start us, length us, event | category | flops | bytes accessed | tf_op | source)
XLA Modules:
  0.0 195.0 jit_solution(952350917226696919)
XLA Ops:
  0.6 9.8 %collective-permute-start.5 = (bf16[3,64,512]{2,1,0:T(8,128)(2,1)}, bf16[3,64,512]{2,1,0:T(8,128)(2,1)S(1)}, u32[]{:S(2)}, u32[]{:S(2)}) collective-permute-start(bf16[3,64,512]{2,1,0:T(8,128)(2,1)} %bitcast.142), channel_id=1, source_target_pairs={{0,8},{8,0},{1,9},{9,1},{2,10},{10,2},{3,11},{11,3},{4,12},{12,4},... | collective-permute-start | bytes 589832 | tf_op jit(solution)/shard_map/ppermute | solution.py:18
  10.4 1.4 fusion.16
  11.8 8.3 %all-gather.1 = f32[4,2,128]{2,1,0:T(2,128)S(1)} all-gather(f32[1,2,128]{2,1,0:T(2,128)S(1)} %maximum_bitcast_fusion), channel_id=2, replica_groups=mesh['zi'=2,'y'=4,'x'=4,'zh'=2,'zl'=4,'c'=2] {'y'}, dimensions={0}, use_global_device_ids=true | all-gather | bytes 5120 | tf_op jit(solution)/shard_map/all_gather | solution.py:80
  20.1 10.3 %collective-permute-start = (f32[2,128]{1,0:T(2,128)S(1)}, f32[2,128]{1,0:T(2,128)S(1)}, u32[]{:S(2)}, u32[]{:S(2)}) collective-permute-start(f32[2,128]{1,0:T(2,128)S(1)} %reduce_sum.47), channel_id=1, source_target_pairs={{0,256},{256,0},{1,257},{257,1},{2,258},{258,2},{3,259},{259,3},{4... | collective-permute-start | bytes 3080 | tf_op jit(solution)/shard_map/ppermute | solution.py:18
  30.6 0.3 copy.46
  30.9 0.9 copy.41
  31.7 7.3 %all-to-all-start.2 = ((bf16[8,128,256]{1,2,0:T(8,128)(2,1)}), bf16[8,128,256]{1,2,0:T(8,128)(2,1)}, u32[]{:S(2)}, u32[]{:S(2)}) async-start(bf16[8,128,256]{1,2,0:T(8,128)(2,1)} %bitcast.34), calls=%async_computation.2 | async-start | bytes 1048576 | tf_op jit(solution)/shard_map/all_to_all | solution.py:53
  39.2 0.3 fusion.29
  39.6 0.2 concatenate.23
  39.8 5.1 %collective-permute-start.3 = (bf16[144,512]{1,0:T(8,128)(2,1)S(1)}, bf16[144,512]{1,0:T(8,128)(2,1)S(1)}, u32[]{:S(2)}, u32[]{:S(2)}) collective-permute-start(bf16[144,512]{1,0:T(8,128)(2,1)S(1)} %concatenate.23), channel_id=1, source_target_pairs={{0,6},{2,4},{4,2},{6,0},{1,7},{3,5},{5,3},{7,1},{8,14},{10,12},{12... | collective-permute-start | bytes 442376 | tf_op jit(solution)/shard_map/ppermute | solution.py:22
  44.9 1.9 collective-permute-start.2
  46.8 2.3 %collective-permute-start.1 = (bf16[144,512]{1,0:T(8,128)(2,1)S(1)}, bf16[144,512]{1,0:T(8,128)(2,1)S(1)}, u32[]{:S(2)}, u32[]{:S(2)}) collective-permute-start(bf16[144,512]{1,0:T(8,128)(2,1)S(1)} %concatenate.23), channel_id=1, source_target_pairs={{0,2},{2,0},{4,6},{6,4},{1,3},{3,1},{5,7},{7,5},{8,10},{10,8},{12,... | collective-permute-start | bytes 442376 | tf_op jit(solution)/shard_map/ppermute | solution.py:22
  49.2 8.3 %collective-permute-done.1 = bf16[144,512]{1,0:T(8,128)(2,1)S(1)} collective-permute-done((bf16[144,512]{1,0:T(8,128)(2,1)S(1)}, bf16[144,512]{1,0:T(8,128)(2,1)S(1)}, u32[]{:S(2)}, u32[]{:S(2)}) %collective-permute-start.1) | collective-permute-done | bytes 147488 | tf_op jit(solution)/shard_map/ppermute | solution.py:22
  57.6 3.1 %collective-permute-start.6 = (bf16[3,2,64,512]{3,2,1,0:T(8,128)(2,1)S(1)}, bf16[3,2,64,512]{3,2,1,0:T(8,128)(2,1)S(1)}, u32[]{:S(2)}, u32[]{:S(2)}) collective-permute-start(bf16[3,2,64,512]{3,2,1,0:T(8,128)(2,1)S(1)} %pad_maximum_fusion.3), channel_id=1, source_target_pairs={{0,16},{16,0},{32,48},{48,32},{1,17},{17,1},{33,49},{49,33},{2,18}... | collective-permute-start | bytes 1179656 | tf_op jit(solution)/shard_map/ppermute | solution.py:22
  60.7 5.4 %collective-permute-done.2 = bf16[144,512]{1,0:T(8,128)(2,1)S(1)} collective-permute-done((bf16[144,512]{1,0:T(8,128)(2,1)S(1)}, bf16[144,512]{1,0:T(8,128)(2,1)S(1)}, u32[]{:S(2)}, u32[]{:S(2)}) %collective-permute-start.2) | collective-permute-done | bytes 147488 | tf_op jit(solution)/shard_map/ppermute | solution.py:22
  66.1 4.7 %collective-permute-start.7 = (bf16[3,2,64,512]{3,2,1,0:T(8,128)(2,1)S(1)}, bf16[3,2,64,512]{3,2,1,0:T(8,128)(2,1)S(1)}, u32[]{:S(2)}, u32[]{:S(2)}) collective-permute-start(bf16[3,2,64,512]{3,2,1,0:T(8,128)(2,1)S(1)} %pad_maximum_fusion.3), channel_id=1, source_target_pairs={{0,32},{16,48},{32,0},{48,16},{1,33},{17,49},{33,1},{49,17},{2,34}... | collective-permute-start | bytes 1179656 | tf_op jit(solution)/shard_map/ppermute | solution.py:22
  70.8 3.2 %collective-permute-start.4 = (bf16[4,144,512]{2,1,0:T(8,128)(2,1)S(1)}, bf16[4,144,512]{2,1,0:T(8,128)(2,1)S(1)}, u32[]{:S(2)}, u32[]{:S(2)}) collective-permute-start(bf16[4,144,512]{2,1,0:T(8,128)(2,1)S(1)} %bitcast_dynamic-update-slice_fusion.4), channel_id=1, source_target_pairs={{0,1},{1,0},{2,3},{3,2},{4,5},{5,4},{6,7},{7,6},{8,9},{9,8},{10,11... | collective-permute-start | bytes 1769480 | tf_op jit(solution)/shard_map/ppermute | solution.py:18
  74.0 2.8 %collective-permute-start.8 = (bf16[3,2,64,512]{3,2,1,0:T(8,128)(2,1)S(1)}, bf16[3,2,64,512]{3,2,1,0:T(8,128)(2,1)S(1)}, u32[]{:S(2)}, u32[]{:S(2)}) collective-permute-start(bf16[3,2,64,512]{3,2,1,0:T(8,128)(2,1)S(1)} %pad_maximum_fusion.3), channel_id=1, source_target_pairs={{0,48},{16,32},{32,16},{48,0},{1,49},{17,33},{33,17},{49,1},{2,50}... | collective-permute-start | bytes 1179656 | tf_op jit(solution)/shard_map/ppermute | solution.py:22
  76.7 0.2 broadcast_in_dim.77
  77.0 3.4 %collective-permute-done.7 = bf16[3,2,64,512]{3,2,1,0:T(8,128)(2,1)S(1)} collective-permute-done((bf16[3,2,64,512]{3,2,1,0:T(8,128)(2,1)S(1)}, bf16[3,2,64,512]{3,2,1,0:T(8,128)(2,1)S(1)}, u32[]{:S(2)}, u32[]{:S(2)}) %collective-permute-start.7) | collective-permute-done | bytes 393248 | tf_op jit(solution)/shard_map/ppermute | solution.py:22
  80.5 9.2 %collective-permute-done.8 = bf16[3,2,64,512]{3,2,1,0:T(8,128)(2,1)S(1)} collective-permute-done((bf16[3,2,64,512]{3,2,1,0:T(8,128)(2,1)S(1)}, bf16[3,2,64,512]{3,2,1,0:T(8,128)(2,1)S(1)}, u32[]{:S(2)}, u32[]{:S(2)}) %collective-permute-start.8) | collective-permute-done | bytes 393248 | tf_op jit(solution)/shard_map/ppermute | solution.py:22
  90.2 0.7 fusion.43
  90.9 0.7 fusion.42
  91.7 1.8 add_convert_fusion
  93.5 4.3 %all-to-all-start = ((bf16[4,128,1024]{2,1,0:T(8,128)(2,1)}), bf16[4,128,1024]{2,1,0:T(8,128)(2,1)}, u32[]{:S(2)}, u32[]{:S(2)}) async-start(bf16[4,128,1024]{2,1,0:T(8,128)(2,1)} %bitcast.129), calls=%async_computation | async-start | bytes 2097152 | tf_op jit(solution)/shard_map/all_to_all | solution.py:113
  97.8 1.2 copy.42
  99.1 3.3 %collective-permute-start.10 = (bf16[1024,256]{1,0:T(8,128)(2,1)S(1)}, bf16[1024,256]{1,0:T(8,128)(2,1)}, u32[]{:S(2)}, u32[]{:S(2)}) collective-permute-start(bf16[1024,256]{1,0:T(8,128)(2,1)S(1)} %bitcast.130), channel_id=1, source_target_pairs={{0,64},{64,0},{128,192},{192,128},{1,65},{65,1},{129,193},{193,129... | collective-permute-start | bytes 1572872 | tf_op jit(solution)/shard_map/ppermute | solution.py:22
  102.4 10.1 %all-to-all-done = bf16[4,128,1024]{2,1,0:T(8,128)(2,1)} async-done(((bf16[4,128,1024]{2,1,0:T(8,128)(2,1)}), bf16[4,128,1024]{2,1,0:T(8,128)(2,1)}, u32[]{:S(2)}, u32[]{:S(2)}) %all-to-all-start) | async-done | bytes 1048608 | tf_op jit(solution)/shard_map/all_to_all | solution.py:113
  112.6 1.5 convert_reduce_fusion
  114.0 8.3 %collective-permute-done.10 = bf16[1024,256]{1,0:T(8,128)(2,1)} collective-permute-done((bf16[1024,256]{1,0:T(8,128)(2,1)S(1)}, bf16[1024,256]{1,0:T(8,128)(2,1)}, u32[]{:S(2)}, u32[]{:S(2)}) %collective-permute-start.10) | collective-permute-done | bytes 524320 | tf_op jit(solution)/shard_map/ppermute | solution.py:22
  122.3 1.1 broadcast_select_fusion.1
  123.4 0.8 convolution_convert_fusion
  124.3 0.8 convolution_convert_fusion.1
  125.1 0.8 convolution_convert_fusion.2
  126.1 1.1 dynamic-slice_bitcast_fusion.2
  127.2 2.5 %collective-permute-start.11 = (bf16[400,512]{1,0:T(8,128)(2,1)}, bf16[400,512]{1,0:T(8,128)(2,1)}, u32[]{:S(2)}, u32[]{:S(2)}) collective-permute-start(bf16[400,512]{1,0:T(8,128)(2,1)} %get-tuple-element.17), channel_id=1, source_target_pairs={{0,16},{16,0},{32,48},{48,32},{1,17},{17,1},{33,49},{49,33},{2,18}... | collective-permute-start | bytes 1228808 | tf_op jit(solution)/shard_map/ppermute | solution.py:22
  129.7 3.8 %collective-permute-start.13 = (bf16[400,512]{1,0:T(8,128)(2,1)}, bf16[400,512]{1,0:T(8,128)(2,1)}, u32[]{:S(2)}, u32[]{:S(2)}) collective-permute-start(bf16[400,512]{1,0:T(8,128)(2,1)} %get-tuple-element.18), channel_id=1, source_target_pairs={{0,48},{16,32},{32,16},{48,0},{1,49},{17,33},{33,17},{49,1},{2,50}... | collective-permute-start | bytes 1228808 | tf_op jit(solution)/shard_map/ppermute | solution.py:22
  133.5 2.7 %collective-permute-start.12 = (bf16[400,512]{1,0:T(8,128)(2,1)}, bf16[400,512]{1,0:T(8,128)(2,1)}, u32[]{:S(2)}, u32[]{:S(2)}) collective-permute-start(bf16[400,512]{1,0:T(8,128)(2,1)} %get-tuple-element.19), channel_id=1, source_target_pairs={{0,32},{16,48},{32,0},{48,16},{1,33},{17,49},{33,1},{49,17},{2,34}... | collective-permute-start | bytes 1228808 | tf_op jit(solution)/shard_map/ppermute | solution.py:22
  136.2 5.2 %collective-permute-start.9 = (bf16[64,1024]{1,0:T(8,128)(2,1)S(1)}, bf16[64,1024]{1,0:T(8,128)(2,1)S(1)}, u32[]{:S(2)}, u32[]{:S(2)}) collective-permute-start(bf16[64,1024]{1,0:T(8,128)(2,1)S(1)} %select_convert_fusion.1), channel_id=1, source_target_pairs={{0,256},{256,0},{1,257},{257,1},{2,258},{258,2},{3,259},{259,3},{4... | collective-permute-start | bytes 393224 | tf_op jit(solution)/shard_map/ppermute | solution.py:18
  141.5 15.1 %collective-permute-done.9 = bf16[64,1024]{1,0:T(8,128)(2,1)S(1)} collective-permute-done((bf16[64,1024]{1,0:T(8,128)(2,1)S(1)}, bf16[64,1024]{1,0:T(8,128)(2,1)S(1)}, u32[]{:S(2)}, u32[]{:S(2)}) %collective-permute-start.9) | collective-permute-done | bytes 131104 | tf_op jit(solution)/shard_map/ppermute | solution.py:18
  156.7 0.7 copy.39
  157.4 8.2 %all-to-all-start.1 = ((bf16[8,64,128]{2,1,0:T(8,128)(2,1)}), bf16[8,64,128]{2,1,0:T(8,128)(2,1)S(1)}, u32[]{:S(2)}, u32[]{:S(2)}) async-start(bf16[8,64,128]{2,1,0:T(8,128)(2,1)} %copy.39), calls=%async_computation.1 | async-start | bytes 262144 | tf_op jit(solution)/shard_map/all_to_all | solution.py:120
  165.6 1.5 fusion.6
  167.2 5.7 %collective-permute-start.14 = (bf16[208,512]{1,0:T(8,128)(2,1)S(1)}, bf16[208,512]{1,0:T(8,128)(2,1)S(1)}, u32[]{:S(2)}, u32[]{:S(2)}) collective-permute-start(bf16[208,512]{1,0:T(8,128)(2,1)S(1)} %pad_maximum_fusion.7), channel_id=1, source_target_pairs={{0,8},{8,0},{1,9},{9,1},{2,10},{10,2},{3,11},{11,3},{4,12},{12,4},... | collective-permute-start | bytes 638984 | tf_op jit(solution)/shard_map/ppermute | solution.py:18
  172.9 0.8 copy.45
  173.6 19.8 %collective-permute-done.14 = bf16[208,512]{1,0:T(8,128)(2,1)S(1)} collective-permute-done((bf16[208,512]{1,0:T(8,128)(2,1)S(1)}, bf16[208,512]{1,0:T(8,128)(2,1)S(1)}, u32[]{:S(2)}, u32[]{:S(2)}) %collective-permute-start.14) | collective-permute-done | bytes 213024 | tf_op jit(solution)/shard_map/ppermute | solution.py:18
  193.5 0.8 fusion.10
  194.4 0.6 fusion.32
  (65 shorter events, 1.5 us)
Async XLA Ops:
  0.6 29.8 %copy-start = (bf16[128,4096]{1,0:T(8,128)(2,1)S(1)}, bf16[128,4096]{1,0:T(8,128)(2,1)}, u32[]{:S(2)}) copy-start(bf16[128,4096]{1,0:T(8,128)(2,1)} %param.6) | copy-start | bytes 3145732
  0.6 56.8 %collective-permute-start.5 = (bf16[3,64,512]{2,1,0:T(8,128)(2,1)}, bf16[3,64,512]{2,1,0:T(8,128)(2,1)S(1)}, u32[]{:S(2)}, u32[]{:S(2)}) collective-permute-start(bf16[3,64,512]{2,1,0:T(8,128)(2,1)} %bitcast.142), channel_id=1, source_target_pairs={{0,8},{8,0},{1,9},{9,1},{2,10},{10,2},{3,11},{11,3},{4,12},{12,4},... | collective-permute-start | bytes 589832 | tf_op jit(solution)/shard_map/ppermute | solution.py:18
  20.1 19.0 %collective-permute-start = (f32[2,128]{1,0:T(2,128)S(1)}, f32[2,128]{1,0:T(2,128)S(1)}, u32[]{:S(2)}, u32[]{:S(2)}) collective-permute-start(f32[2,128]{1,0:T(2,128)S(1)} %reduce_sum.47), channel_id=1, source_target_pairs={{0,256},{256,0},{1,257},{257,1},{2,258},{258,2},{3,259},{259,3},{4... | collective-permute-start | bytes 3080 | tf_op jit(solution)/shard_map/ppermute | solution.py:18
  30.5 8.5 %copy-start.4 = (s32[128]{0:T(128)S(1)}, s32[128]{0:T(128)}, u32[]{:S(2)}) copy-start(s32[128]{0:T(128)} %param.9) | copy-start | bytes 1540
  30.5 8.6 %copy-start.1 = (bf16[128,512]{1,0:T(8,128)(2,1)S(1)}, bf16[128,512]{1,0:T(8,128)(2,1)}, u32[]{:S(2)}) copy-start(bf16[128,512]{1,0:T(8,128)(2,1)} %param.7) | copy-start | bytes 393220
  30.5 8.6 %copy-start.3 = (bf16[128,512]{1,0:T(8,128)(2,1)S(1)}, bf16[128,512]{1,0:T(8,128)(2,1)}, u32[]{:S(2)}) copy-start(bf16[128,512]{1,0:T(8,128)(2,1)} %param.8) | copy-start | bytes 393220
  30.8 26.6 %copy-start.2 = (bf16[64,3,512]{2,0,1:T(8,128)(2,1)S(1)}, bf16[64,3,512]{2,0,1:T(8,128)(2,1)}, u32[]{:S(2)}) copy-start(bf16[64,3,512]{2,0,1:T(8,128)(2,1)} %param.10) | copy-start | bytes 589828
  31.7 61.8 %all-to-all-start.2 = ((bf16[8,128,256]{1,2,0:T(8,128)(2,1)}), bf16[8,128,256]{1,2,0:T(8,128)(2,1)}, u32[]{:S(2)}, u32[]{:S(2)}) async-start(bf16[8,128,256]{1,2,0:T(8,128)(2,1)} %bitcast.34), calls=%async_computation.2 | async-start | bytes 1048576 | tf_op jit(solution)/shard_map/all_to_all | solution.py:53
  39.8 31.0 %collective-permute-start.3 = (bf16[144,512]{1,0:T(8,128)(2,1)S(1)}, bf16[144,512]{1,0:T(8,128)(2,1)S(1)}, u32[]{:S(2)}, u32[]{:S(2)}) collective-permute-start(bf16[144,512]{1,0:T(8,128)(2,1)S(1)} %concatenate.23), channel_id=1, source_target_pairs={{0,6},{2,4},{4,2},{6,0},{1,7},{3,5},{5,3},{7,1},{8,14},{10,12},{12... | collective-permute-start | bytes 442376 | tf_op jit(solution)/shard_map/ppermute | solution.py:22
  44.9 21.2 %collective-permute-start.2 = (bf16[144,512]{1,0:T(8,128)(2,1)S(1)}, bf16[144,512]{1,0:T(8,128)(2,1)S(1)}, u32[]{:S(2)}, u32[]{:S(2)}) collective-permute-start(bf16[144,512]{1,0:T(8,128)(2,1)S(1)} %concatenate.23), channel_id=1, source_target_pairs={{0,4},{2,6},{4,0},{6,2},{1,5},{3,7},{5,1},{7,3},{8,12},{10,14},{12... | collective-permute-start | bytes 442376 | tf_op jit(solution)/shard_map/ppermute | solution.py:22
  46.8 10.6 %collective-permute-start.1 = (bf16[144,512]{1,0:T(8,128)(2,1)S(1)}, bf16[144,512]{1,0:T(8,128)(2,1)S(1)}, u32[]{:S(2)}, u32[]{:S(2)}) collective-permute-start(bf16[144,512]{1,0:T(8,128)(2,1)S(1)} %concatenate.23), channel_id=1, source_target_pairs={{0,2},{2,0},{4,6},{6,4},{1,3},{3,1},{5,7},{7,5},{8,10},{10,8},{12,... | collective-permute-start | bytes 442376 | tf_op jit(solution)/shard_map/ppermute | solution.py:22
  57.6 19.4 %collective-permute-start.6 = (bf16[3,2,64,512]{3,2,1,0:T(8,128)(2,1)S(1)}, bf16[3,2,64,512]{3,2,1,0:T(8,128)(2,1)S(1)}, u32[]{:S(2)}, u32[]{:S(2)}) collective-permute-start(bf16[3,2,64,512]{3,2,1,0:T(8,128)(2,1)S(1)} %pad_maximum_fusion.3), channel_id=1, source_target_pairs={{0,16},{16,0},{32,48},{48,32},{1,17},{17,1},{33,49},{49,33},{2,18}... | collective-permute-start | bytes 1179656 | tf_op jit(solution)/shard_map/ppermute | solution.py:22
  66.1 14.3 %collective-permute-start.7 = (bf16[3,2,64,512]{3,2,1,0:T(8,128)(2,1)S(1)}, bf16[3,2,64,512]{3,2,1,0:T(8,128)(2,1)S(1)}, u32[]{:S(2)}, u32[]{:S(2)}) collective-permute-start(bf16[3,2,64,512]{3,2,1,0:T(8,128)(2,1)S(1)} %pad_maximum_fusion.3), channel_id=1, source_target_pairs={{0,32},{16,48},{32,0},{48,16},{1,33},{17,49},{33,1},{49,17},{2,34}... | collective-permute-start | bytes 1179656 | tf_op jit(solution)/shard_map/ppermute | solution.py:22
  70.8 19.0 %collective-permute-start.4 = (bf16[4,144,512]{2,1,0:T(8,128)(2,1)S(1)}, bf16[4,144,512]{2,1,0:T(8,128)(2,1)S(1)}, u32[]{:S(2)}, u32[]{:S(2)}) collective-permute-start(bf16[4,144,512]{2,1,0:T(8,128)(2,1)S(1)} %bitcast_dynamic-update-slice_fusion.4), channel_id=1, source_target_pairs={{0,1},{1,0},{2,3},{3,2},{4,5},{5,4},{6,7},{7,6},{8,9},{9,8},{10,11... | collective-permute-start | bytes 1769480 | tf_op jit(solution)/shard_map/ppermute | solution.py:18
  74.0 15.7 %collective-permute-start.8 = (bf16[3,2,64,512]{3,2,1,0:T(8,128)(2,1)S(1)}, bf16[3,2,64,512]{3,2,1,0:T(8,128)(2,1)S(1)}, u32[]{:S(2)}, u32[]{:S(2)}) collective-permute-start(bf16[3,2,64,512]{3,2,1,0:T(8,128)(2,1)S(1)} %pad_maximum_fusion.3), channel_id=1, source_target_pairs={{0,48},{16,32},{32,16},{48,0},{1,49},{17,33},{33,17},{49,1},{2,50}... | collective-permute-start | bytes 1179656 | tf_op jit(solution)/shard_map/ppermute | solution.py:22
  93.5 19.1 %all-to-all-start = ((bf16[4,128,1024]{2,1,0:T(8,128)(2,1)}), bf16[4,128,1024]{2,1,0:T(8,128)(2,1)}, u32[]{:S(2)}, u32[]{:S(2)}) async-start(bf16[4,128,1024]{2,1,0:T(8,128)(2,1)} %bitcast.129), calls=%async_computation | async-start | bytes 2097152 | tf_op jit(solution)/shard_map/all_to_all | solution.py:113
  99.1 23.2 %collective-permute-start.10 = (bf16[1024,256]{1,0:T(8,128)(2,1)S(1)}, bf16[1024,256]{1,0:T(8,128)(2,1)}, u32[]{:S(2)}, u32[]{:S(2)}) collective-permute-start(bf16[1024,256]{1,0:T(8,128)(2,1)S(1)} %bitcast.130), channel_id=1, source_target_pairs={{0,64},{64,0},{128,192},{192,128},{1,65},{65,1},{129,193},{193,129... | collective-permute-start | bytes 1572872 | tf_op jit(solution)/shard_map/ppermute | solution.py:22
  127.2 38.4 %collective-permute-start.11 = (bf16[400,512]{1,0:T(8,128)(2,1)}, bf16[400,512]{1,0:T(8,128)(2,1)}, u32[]{:S(2)}, u32[]{:S(2)}) collective-permute-start(bf16[400,512]{1,0:T(8,128)(2,1)} %get-tuple-element.17), channel_id=1, source_target_pairs={{0,16},{16,0},{32,48},{48,32},{1,17},{17,1},{33,49},{49,33},{2,18}... | collective-permute-start | bytes 1228808 | tf_op jit(solution)/shard_map/ppermute | solution.py:22
  129.7 35.8 %collective-permute-start.13 = (bf16[400,512]{1,0:T(8,128)(2,1)}, bf16[400,512]{1,0:T(8,128)(2,1)}, u32[]{:S(2)}, u32[]{:S(2)}) collective-permute-start(bf16[400,512]{1,0:T(8,128)(2,1)} %get-tuple-element.18), channel_id=1, source_target_pairs={{0,48},{16,32},{32,16},{48,0},{1,49},{17,33},{33,17},{49,1},{2,50}... | collective-permute-start | bytes 1228808 | tf_op jit(solution)/shard_map/ppermute | solution.py:22
  133.5 32.1 %collective-permute-start.12 = (bf16[400,512]{1,0:T(8,128)(2,1)}, bf16[400,512]{1,0:T(8,128)(2,1)}, u32[]{:S(2)}, u32[]{:S(2)}) collective-permute-start(bf16[400,512]{1,0:T(8,128)(2,1)} %get-tuple-element.19), channel_id=1, source_target_pairs={{0,32},{16,48},{32,0},{48,16},{1,33},{17,49},{33,1},{49,17},{2,34}... | collective-permute-start | bytes 1228808 | tf_op jit(solution)/shard_map/ppermute | solution.py:22
  136.2 20.4 %collective-permute-start.9 = (bf16[64,1024]{1,0:T(8,128)(2,1)S(1)}, bf16[64,1024]{1,0:T(8,128)(2,1)S(1)}, u32[]{:S(2)}, u32[]{:S(2)}) collective-permute-start(bf16[64,1024]{1,0:T(8,128)(2,1)S(1)} %select_convert_fusion.1), channel_id=1, source_target_pairs={{0,256},{256,0},{1,257},{257,1},{2,258},{258,2},{3,259},{259,3},{4... | collective-permute-start | bytes 393224 | tf_op jit(solution)/shard_map/ppermute | solution.py:18
  157.4 15.5 %all-to-all-start.1 = ((bf16[8,64,128]{2,1,0:T(8,128)(2,1)}), bf16[8,64,128]{2,1,0:T(8,128)(2,1)S(1)}, u32[]{:S(2)}, u32[]{:S(2)}) async-start(bf16[8,64,128]{2,1,0:T(8,128)(2,1)} %copy.39), calls=%async_computation.1 | async-start | bytes 262144 | tf_op jit(solution)/shard_map/all_to_all | solution.py:120
  167.2 26.3 %collective-permute-start.14 = (bf16[208,512]{1,0:T(8,128)(2,1)S(1)}, bf16[208,512]{1,0:T(8,128)(2,1)S(1)}, u32[]{:S(2)}, u32[]{:S(2)}) collective-permute-start(bf16[208,512]{1,0:T(8,128)(2,1)S(1)} %pad_maximum_fusion.7), channel_id=1, source_target_pairs={{0,8},{8,0},{1,9},{9,1},{2,10},{10,2},{3,11},{11,3},{4,12},{12,4},... | collective-permute-start | bytes 638984 | tf_op jit(solution)/shard_map/ppermute | solution.py:18

commit v3 on v2

--- a/solution.py
+++ b/solution.py
@@ -44,7 +44,7 @@
     width = cols * lax.axis_size(DP)
     xs, ys = lax.axis_size("x"), lax.axis_size("y")
     members = lax.axis_size(GROUP)
-    x, y, zh, zl, c, zi = (lax.axis_index(a) for a in ("x", "y", "zh", "zl", "c", "zi"))
+    x, y, zh, c, zi = (lax.axis_index(a) for a in ("x", "y", "zh", "c", "zi"))
     blocks = feats // (members * rows)
 
     feature_rows = lax.dynamic_slice_in_dim(context, (y & 1) * (feats // 2), feats // 2, 1)
@@ -93,12 +93,10 @@
         [grad_proj, two_terms(gain_terms), mod_row, jnp.zeros((spare, cols), BF16)], axis=0
     )
     line = lax.axis_size("zl")
-    near = jnp.zeros((line, *packet.shape), BF16)
-    for k in range(line):
-        piece = packet if k == 0 else crossed(packet, "zl", k)
-        near = lax.dynamic_update_index_in_dim(near, piece, zl ^ k, 0)
-    others = swap(near, "c")
-    packets = in_order(c, near, others, 1).reshape(members, tok + 16, cols)
+    packets = jnp.broadcast_to(packet[None], (line, *packet.shape))
+    packets = lax.all_to_all(packets, "zl", 0, 0, tiled=True)
+    others = swap(packets, "c")
+    packets = in_order(c, packets, others, 1).reshape(members, tok + 16, cols)
     grads = packets[:, :tok].reshape(members * tok, cols)
     gain_part = jnp.sum(joined_terms(packets[:, tok:], towers), axis=0)
     ids = packets[:, tok + 2 * towers, :tok].astype(jnp.int32).reshape(members * tok)
@@ -110,8 +108,13 @@
         )
         partial = partial + (ids == m).astype(F32)[None, :] * product
     partial = partial.astype(BF16).reshape(ys, 2 * rows, members * tok)
-    partial = lax.all_to_all(partial, "y", 0, 0, tiled=True)
-    partial = jnp.sum(partial.astype(F32), axis=0).reshape(2, rows, members * tok)
+    parts = []
+    for k in range(ys):
+        part = lax.dynamic_index_in_dim(partial, y ^ k, 0, keepdims=False)
+        parts.append(part if k == 0 else crossed(part, "y", k))
+    parts = [part.astype(F32) for part in parts]
+    partial = (parts[0] + parts[1]) + (parts[2] + parts[3])
+    partial = partial.reshape(2, rows, members * tok)
     kept = jnp.where(zi == 0, partial[0], partial[1])
     sent = jnp.where(zi == 0, partial[1], partial[0]).astype(BF16)
     got = swap(sent, "zi")
@@ -131,13 +134,9 @@
     gain_rows = jnp.pad(two_terms(gain_part), ((0, 16 - 2 * towers), (0, 0)))
     updates.append(jnp.broadcast_to(gain_rows[None], (xs, 16, cols)))
     updates = jnp.concatenate(updates, axis=1)
-    parts = []
-    for k in range(xs):
-        part = lax.dynamic_index_in_dim(updates, x ^ k, 0, keepdims=False)
-        parts.append(part if k == 0 else crossed(part, "x", k))
+    updates = lax.all_to_all(updates, "x", 0, 0, tiled=True)
     size = towers * 2 * rows
-    parts = [part.astype(F32) for part in parts]
-    total_part = (parts[0] + parts[1]) + (parts[2] + parts[3])
+    total_part = jnp.sum(updates.astype(F32), axis=0)
     weight_part = total_part[:size].reshape(towers, 2, rows, cols)
     gain_part = joined_terms(total_part[size:], towers)
     kept = jnp.where(zh == 0, weight_part[:, 0], weight_part[:, 1])

time: 196 us -> 192 us (0.980)
  waiting for transfers between devices: 79.6 us -> 45.6 us
  starting transfers between devices: 86 us -> 111 us
  local copies, waits for them, and re-layouts: 5.83 us -> 12.8 us
  blocking collectives: 8.27 us -> 5.25 us
  other arithmetic: 6.39 us -> 9.21 us
  matrix products: 7.55 us -> 5.56 us
    ppermute x10 -> x7, waiting for transfers between devices: 34.5 us -> 14.2 us  [crossed(): lax.ppermute(value, axis, [(i, i ^ k) for i in range(lax.axis_size(axis))])]
    all_to_all x1, starting transfers between devices: 8.2 us -> 23.8 us  [local(): settled = lax.all_to_all(total, GROUP, 0, 0, tiled=True)]
    ppermute x5, starting transfers between devices: 34.2 us -> 46.5 us  [swap(): return lax.ppermute(value, axis, [(0, 1), (1, 0)])]
    ppermute x10 -> x7, starting transfers between devices: 32.1 us -> 21.1 us  [crossed(): lax.ppermute(value, axis, [(i, i ^ k) for i in range(lax.axis_size(axis))])]
    all_to_all x1 -> x2, waiting for transfers between devices: 10.1 us -> 0.01 us  [the longest x1 0.01 us: local(): packets = lax.all_to_all(packets, 'zl', 0, 0, tiled=True)]
    ppermute x5, waiting for transfers between devices: 35 us -> 29.9 us  [swap(): return lax.ppermute(value, axis, [(0, 1), (1, 0)])]
    all_to_all x1 -> x2, starting transfers between devices: 4.27 us -> 9.24 us  [the longest x1 4.75 us: local(): packets = lax.all_to_all(packets, 'zl', 0, 0, tiled=True)]
    all_to_all x1, starting transfers between devices: 7.28 us -> 10.4 us  [local(): half = lax.all_to_all(feature_rows, GROUP, 0, 0, tiled=True)]
  transfers between devices with their start and end apart: 18 -> 16, of which waited for: 8 -> 8; matrix products, arithmetic and copies ran while one was open for 7% -> 9% of each run, Pallas kernels for 0% -> 0%
where the time goes in v3:
time: 192 us; the launch traced here: 191 us
  starting transfers between devices  111 us (58%)
  waiting for transfers between devices  45.6 us (24%)
  local copies, waits for them, and re-layouts  12.8 us (7%)
  other arithmetic  9.21 us (5%)
  matrix products  5.56 us (3%)
  blocking collectives  5.25 us (3%)
    ppermute x5, starting transfers between devices, swap(): return lax.ppermute(value, axis, [(0, 1), (1, 0)])  46.5 us
    ppermute x5, waiting for transfers between devices, swap(): return lax.ppermute(value, axis, [(0, 1), (1, 0)])  29.9 us
    all_to_all x1, starting transfers between devices, local(): settled = lax.all_to_all(total, GROUP, 0, 0, tiled=True)  23.8 us
    ppermute x7, starting transfers between devices, crossed(): lax.ppermute(value, axis, [(i, i ^ k) for i in range(lax.axis_size(axis))])  21.1 us
    ppermute x7, waiting for transfers between devices, crossed(): lax.ppermute(value, axis, [(i, i ^ k) for i in range(lax.axis_size(axis))])  14.2 us
    all_to_all x1, starting transfers between devices, local(): half = lax.all_to_all(feature_rows, GROUP, 0, 0, tiled=True)  10.4 us
    all_gather x1, blocking collectives, local(): stats = lax.all_gather(stats, 'y')  5.25 us
    all_to_all x1, starting transfers between devices, local(): packets = lax.all_to_all(packets, 'zl', 0, 0, tiled=True)  4.75 us
  transfers between devices with their start and end apart: 16, of which 8 were waited for; matrix products, arithmetic and copies ran while one was open for 9% of the time, Pallas kernels for 0%

profile of v3, /device:TPU:1, one launch (start us, length us, event | category | flops | bytes accessed | tf_op | source)
XLA Modules:
  0.0 190.5 jit_solution(10460232884320125220)
XLA Ops:
  0.7 1.2 copy-done
  2.2 0.8 copy.41
  3.0 10.4 %all-to-all-start.2 = ((bf16[8,128,256]{1,2,0:T(8,128)(2,1)}), bf16[8,128,256]{1,2,0:T(8,128)(2,1)S(1)}, u32[]{:S(2)}, u32[]{:S(2)}) async-start(bf16[8,128,256]{1,2,0:T(8,128)(2,1)} %bitcast.34), calls=%async_computation.2 | async-start | bytes 1048576 | tf_op jit(solution)/shard_map/all_to_all | solution.py:53
  13.9 5.3 %all-gather.1 = f32[4,2,128]{2,1,0:T(2,128)S(1)} all-gather(f32[1,2,128]{2,1,0:T(2,128)S(1)} %maximum_bitcast_fusion), channel_id=2, replica_groups=mesh['zi'=2,'y'=4,'x'=4,'zh'=2,'zl'=4,'c'=2] {'y'}, dimensions={0}, use_global_device_ids=true | all-gather | bytes 5120 | tf_op jit(solution)/shard_map/all_gather | solution.py:80
  19.1 12.8 %collective-permute-start = (f32[2,128]{1,0:T(2,128)S(1)}, f32[2,128]{1,0:T(2,128)S(1)}, u32[]{:S(2)}, u32[]{:S(2)}) collective-permute-start(f32[2,128]{1,0:T(2,128)S(1)} %reduce_sum.47), channel_id=1, source_target_pairs={{0,256},{256,0},{1,257},{257,1},{2,258},{258,2},{3,259},{259,3},{4... | collective-permute-start | bytes 3080 | tf_op jit(solution)/shard_map/ppermute | solution.py:18
  32.0 0.9 collective-permute-done
  33.6 0.9 broadcast_in_dim.62
  34.6 4.8 %all-to-all-start = ((bf16[4,144,512]{2,1,0:T(8,128)(2,1)}), bf16[4,144,512]{2,1,0:T(8,128)(2,1)S(1)}, u32[]{:S(2)}, u32[]{:S(2)}) async-start(bf16[4,144,512]{2,1,0:T(8,128)(2,1)} %broadcast_in_dim.62), calls=%async_computation | async-start | bytes 1179648 | tf_op jit(solution)/shard_map/all_to_all | solution.py:97
  39.3 7.9 %collective-permute-start.2 = (bf16[3,64,512]{2,1,0:T(8,128)(2,1)S(1)}, bf16[3,64,512]{2,1,0:T(8,128)(2,1)S(1)}, u32[]{:S(2)}, u32[]{:S(2)}) collective-permute-start(bf16[3,64,512]{2,1,0:T(8,128)(2,1)S(1)} %bitcast.135), channel_id=1, source_target_pairs={{0,8},{8,0},{1,9},{9,1},{2,10},{10,2},{3,11},{11,3},{4,12},{12,4},... | collective-permute-start | bytes 589832 | tf_op jit(solution)/shard_map/ppermute | solution.py:18
  47.2 4.4 %collective-permute-done.2 = bf16[3,64,512]{2,1,0:T(8,128)(2,1)S(1)} collective-permute-done((bf16[3,64,512]{2,1,0:T(8,128)(2,1)S(1)}, bf16[3,64,512]{2,1,0:T(8,128)(2,1)S(1)}, u32[]{:S(2)}, u32[]{:S(2)}) %collective-permute-start.2) | collective-permute-done | bytes 196640 | tf_op jit(solution)/shard_map/ppermute | solution.py:18
  52.4 0.8 pad_maximum_fusion.3
  53.2 3.1 %collective-permute-start.3 = (bf16[3,2,64,512]{3,2,1,0:T(8,128)(2,1)}, bf16[3,2,64,512]{3,2,1,0:T(8,128)(2,1)}, u32[]{:S(2)}, u32[]{:S(2)}) collective-permute-start(bf16[3,2,64,512]{3,2,1,0:T(8,128)(2,1)} %pad_maximum_fusion.3), channel_id=1, source_target_pairs={{0,16},{16,0},{32,48},{48,32},{1,17},{17,1},{33,49},{49,33},{2,18}... | collective-permute-start | bytes 1179656 | tf_op jit(solution)/shard_map/ppermute | solution.py:22
  56.3 4.4 %collective-permute-start.4 = (bf16[3,2,64,512]{3,2,1,0:T(8,128)(2,1)}, bf16[3,2,64,512]{3,2,1,0:T(8,128)(2,1)}, u32[]{:S(2)}, u32[]{:S(2)}) collective-permute-start(bf16[3,2,64,512]{3,2,1,0:T(8,128)(2,1)} %pad_maximum_fusion.3), channel_id=1, source_target_pairs={{0,32},{16,48},{32,0},{48,16},{1,33},{17,49},{33,1},{49,17},{2,34}... | collective-permute-start | bytes 1179656 | tf_op jit(solution)/shard_map/ppermute | solution.py:22
  60.7 2.1 %collective-permute-start.5 = (bf16[3,2,64,512]{3,2,1,0:T(8,128)(2,1)}, bf16[3,2,64,512]{3,2,1,0:T(8,128)(2,1)}, u32[]{:S(2)}, u32[]{:S(2)}) collective-permute-start(bf16[3,2,64,512]{3,2,1,0:T(8,128)(2,1)} %pad_maximum_fusion.3), channel_id=1, source_target_pairs={{0,48},{16,32},{32,16},{48,0},{1,49},{17,33},{33,17},{49,1},{2,50}... | collective-permute-start | bytes 1179656 | tf_op jit(solution)/shard_map/ppermute | solution.py:22
  63.0 1.0 bitcast_dynamic-update-slice_fusion.2
  64.0 1.0 bitcast_dynamic-update-slice_fusion.1
  65.0 2.0 %copy.42 = bf16[8,128,256]{2,1,0:T(8,128)(2,1)} copy(bf16[8,128,256]{1,2,0:T(8,128)(2,1)} %copy-done.2) | data formatting | bytes 1048576 | tf_op jit(solution)/shard_map/all_to_all | solution.py:53
  67.0 1.9 %collective-permute-start.10 = (bf16[1024,256]{1,0:T(8,128)(2,1)}, bf16[1024,256]{1,0:T(8,128)(2,1)}, u32[]{:S(2)}, u32[]{:S(2)}) collective-permute-start(bf16[1024,256]{1,0:T(8,128)(2,1)} %bitcast.123), channel_id=1, source_target_pairs={{0,64},{64,0},{128,192},{192,128},{1,65},{65,1},{129,193},{193,129... | collective-permute-start | bytes 1572872 | tf_op jit(solution)/shard_map/ppermute | solution.py:22
  69.0 3.6 %collective-permute-done.4 = bf16[3,2,64,512]{3,2,1,0:T(8,128)(2,1)} collective-permute-done((bf16[3,2,64,512]{3,2,1,0:T(8,128)(2,1)}, bf16[3,2,64,512]{3,2,1,0:T(8,128)(2,1)}, u32[]{:S(2)}, u32[]{:S(2)}) %collective-permute-start.4) | collective-permute-done | bytes 393248 | tf_op jit(solution)/shard_map/ppermute | solution.py:22
  72.6 1.0 bitcast_dynamic-update-slice_fusion
  73.7 7.0 %collective-permute-start.1 = (bf16[4,144,512]{2,1,0:T(8,128)(2,1)S(1)}, bf16[4,144,512]{2,1,0:T(8,128)(2,1)S(1)}, u32[]{:S(2)}, u32[]{:S(2)}) collective-permute-start(bf16[4,144,512]{2,1,0:T(8,128)(2,1)S(1)} %all-to-all-done), channel_id=1, source_target_pairs={{0,1},{1,0},{2,3},{3,2},{4,5},{5,4},{6,7},{7,6},{8,9},{9,8},{10,11... | collective-permute-start | bytes 1769480 | tf_op jit(solution)/shard_map/ppermute | solution.py:18
  80.7 1.0 bitcast_dynamic-update-slice_fusion.3
  81.8 1.2 fusion.41
  83.0 1.1 broadcast_select_fusion.1
  84.5 0.9 convolution_convert_fusion.2
  85.4 0.9 convolution_convert_fusion.1
  86.2 0.8 convolution_convert_fusion
  87.2 1.3 pad_maximum_fusion
  88.5 4.5 %all-to-all-start.3 = ((bf16[4,400,512]{2,1,0:T(8,128)(2,1)}), bf16[4,400,512]{2,1,0:T(8,128)(2,1)}, u32[]{:S(2)}, u32[]{:S(2)}) async-start(bf16[4,400,512]{2,1,0:T(8,128)(2,1)} %pad_maximum_fusion), calls=%async_computation.3 | async-start | bytes 3276800 | tf_op jit(solution)/shard_map/all_to_all | solution.py:137
  93.0 0.7 fusion.42
  94.0 0.7 fusion.43
  94.8 0.8 add_convert_fusion
  95.7 2.1 %collective-permute-start.6 = (bf16[128,1024]{1,0:T(8,128)(2,1)S(1)}, bf16[128,1024]{1,0:T(8,128)(2,1)S(1)}, u32[]{:S(2)}, u32[]{:S(2)}) collective-permute-start(bf16[128,1024]{1,0:T(8,128)(2,1)S(1)} %get-tuple-element.24), channel_id=1, source_target_pairs={{0,64},{64,0},{128,192},{192,128},{1,65},{65,1},{129,193},{193,129... | collective-permute-start | bytes 786440 | tf_op jit(solution)/shard_map/ppermute | solution.py:22
  97.9 2.9 %collective-permute-start.7 = (bf16[128,1024]{1,0:T(8,128)(2,1)S(1)}, bf16[128,1024]{1,0:T(8,128)(2,1)S(1)}, u32[]{:S(2)}, u32[]{:S(2)}) collective-permute-start(bf16[128,1024]{1,0:T(8,128)(2,1)S(1)} %get-tuple-element.26), channel_id=1, source_target_pairs={{0,128},{64,192},{128,0},{192,64},{1,129},{65,193},{129,1},{193,65... | collective-permute-start | bytes 786440 | tf_op jit(solution)/shard_map/ppermute | solution.py:22
  100.8 4.6 %collective-permute-start.8 = (bf16[128,1024]{1,0:T(8,128)(2,1)S(1)}, bf16[128,1024]{1,0:T(8,128)(2,1)}, u32[]{:S(2)}, u32[]{:S(2)}) collective-permute-start(bf16[128,1024]{1,0:T(8,128)(2,1)S(1)} %get-tuple-element.25), channel_id=1, source_target_pairs={{0,192},{64,128},{128,64},{192,0},{1,193},{65,129},{129,65},{193,1... | collective-permute-start | bytes 786440 | tf_op jit(solution)/shard_map/ppermute | solution.py:22
  105.3 4.4 %collective-permute-done.7 = bf16[128,1024]{1,0:T(8,128)(2,1)S(1)} collective-permute-done((bf16[128,1024]{1,0:T(8,128)(2,1)S(1)}, bf16[128,1024]{1,0:T(8,128)(2,1)S(1)}, u32[]{:S(2)}, u32[]{:S(2)}) %collective-permute-start.7) | collective-permute-done | bytes 262176 | tf_op jit(solution)/shard_map/ppermute | solution.py:22
  109.7 6.2 %collective-permute-done.8 = bf16[128,1024]{1,0:T(8,128)(2,1)} collective-permute-done((bf16[128,1024]{1,0:T(8,128)(2,1)S(1)}, bf16[128,1024]{1,0:T(8,128)(2,1)}, u32[]{:S(2)}, u32[]{:S(2)}) %collective-permute-start.8) | collective-permute-done | bytes 262176 | tf_op jit(solution)/shard_map/ppermute | solution.py:22
  115.9 1.1 fusion.6
  117.0 16.3 %collective-permute-start.9 = (bf16[64,1024]{1,0:T(8,128)(2,1)S(1)}, bf16[64,1024]{1,0:T(8,128)(2,1)S(1)}, u32[]{:S(2)}, u32[]{:S(2)}) collective-permute-start(bf16[64,1024]{1,0:T(8,128)(2,1)S(1)} %select_convert_fusion.1), channel_id=1, source_target_pairs={{0,256},{256,0},{1,257},{257,1},{2,258},{258,2},{3,259},{259,3},{4... | collective-permute-start | bytes 393224 | tf_op jit(solution)/shard_map/ppermute | solution.py:18
  133.4 2.9 %collective-permute-done.9 = bf16[64,1024]{1,0:T(8,128)(2,1)S(1)} collective-permute-done((bf16[64,1024]{1,0:T(8,128)(2,1)S(1)}, bf16[64,1024]{1,0:T(8,128)(2,1)S(1)}, u32[]{:S(2)}, u32[]{:S(2)}) %collective-permute-start.9) | collective-permute-done | bytes 131104 | tf_op jit(solution)/shard_map/ppermute | solution.py:18
  136.3 0.7 copy.39
  137.0 23.8 %all-to-all-start.1 = ((bf16[8,64,128]{2,1,0:T(8,128)(2,1)}), bf16[8,64,128]{2,1,0:T(8,128)(2,1)S(1)}, u32[]{:S(2)}, u32[]{:S(2)}) async-start(bf16[8,64,128]{2,1,0:T(8,128)(2,1)} %copy.39), calls=%async_computation.1 | async-start | bytes 262144 | tf_op jit(solution)/shard_map/all_to_all | solution.py:123
  160.8 1.8 convert_reduce_fusion
  162.7 2.4 %collective-permute-start.11 = (bf16[208,512]{1,0:T(8,128)(2,1)S(1)}, bf16[208,512]{1,0:T(8,128)(2,1)S(1)}, u32[]{:S(2)}, u32[]{:S(2)}) collective-permute-start(bf16[208,512]{1,0:T(8,128)(2,1)S(1)} %pad_maximum_fusion.7), channel_id=1, source_target_pairs={{0,8},{8,0},{1,9},{9,1},{2,10},{10,2},{3,11},{11,3},{4,12},{12,4},... | collective-permute-start | bytes 638984 | tf_op jit(solution)/shard_map/ppermute | solution.py:18
  165.2 1.4 all-to-all-done.1
  166.6 0.8 copy.45
  167.4 21.7 %collective-permute-done.11 = bf16[208,512]{1,0:T(8,128)(2,1)S(1)} collective-permute-done((bf16[208,512]{1,0:T(8,128)(2,1)S(1)}, bf16[208,512]{1,0:T(8,128)(2,1)S(1)}, u32[]{:S(2)}, u32[]{:S(2)}) %collective-permute-start.11) | collective-permute-done | bytes 213024 | tf_op jit(solution)/shard_map/ppermute | solution.py:18
  189.1 0.8 fusion.10
  (71 shorter events, 4.0 us)
Async XLA Ops:
  0.6 1.2 copy-start
  1.9 11.5 %copy-start.7 = (bf16[128,512]{1,0:T(8,128)(2,1)S(1)}, bf16[128,512]{1,0:T(8,128)(2,1)}, u32[]{:S(2)}) copy-start(bf16[128,512]{1,0:T(8,128)(2,1)} %param.7) | copy-start | bytes 393220
  1.9 11.5 %copy-start.9 = (bf16[128,512]{1,0:T(8,128)(2,1)S(1)}, bf16[128,512]{1,0:T(8,128)(2,1)}, u32[]{:S(2)}) copy-start(bf16[128,512]{1,0:T(8,128)(2,1)} %param.8) | copy-start | bytes 393220
  1.9 11.5 %copy-start.10 = (f32[3,512]{1,0:T(4,128)S(1)}, f32[3,512]{1,0:T(4,128)}, u32[]{:S(2)}) copy-start(f32[3,512]{1,0:T(4,128)} %param.11) | copy-start | bytes 18436
  1.9 11.6 %copy-start.11 = (s32[128]{0:T(128)S(1)}, s32[128]{0:T(128)}, u32[]{:S(2)}) copy-start(s32[128]{0:T(128)} %param.9) | copy-start | bytes 1540
  3.0 36.3 %copy-start.8 = (bf16[64,3,512]{2,0,1:T(8,128)(2,1)S(1)}, bf16[64,3,512]{2,0,1:T(8,128)(2,1)}, u32[]{:S(2)}) copy-start(bf16[64,3,512]{2,0,1:T(8,128)(2,1)} %param.10) | copy-start | bytes 589828
  3.0 30.5 %all-to-all-start.2 = ((bf16[8,128,256]{1,2,0:T(8,128)(2,1)}), bf16[8,128,256]{1,2,0:T(8,128)(2,1)S(1)}, u32[]{:S(2)}, u32[]{:S(2)}) async-start(bf16[8,128,256]{1,2,0:T(8,128)(2,1)} %bitcast.34), calls=%async_computation.2 | async-start | bytes 1048576 | tf_op jit(solution)/shard_map/all_to_all | solution.py:53
  19.1 13.8 %collective-permute-start = (f32[2,128]{1,0:T(2,128)S(1)}, f32[2,128]{1,0:T(2,128)S(1)}, u32[]{:S(2)}, u32[]{:S(2)}) collective-permute-start(f32[2,128]{1,0:T(2,128)S(1)} %reduce_sum.47), channel_id=1, source_target_pairs={{0,256},{256,0},{1,257},{257,1},{2,258},{258,2},{3,259},{259,3},{4... | collective-permute-start | bytes 3080 | tf_op jit(solution)/shard_map/ppermute | solution.py:18
  33.6 1.0 copy-start.2
  34.6 39.1 %all-to-all-start = ((bf16[4,144,512]{2,1,0:T(8,128)(2,1)}), bf16[4,144,512]{2,1,0:T(8,128)(2,1)S(1)}, u32[]{:S(2)}, u32[]{:S(2)}) async-start(bf16[4,144,512]{2,1,0:T(8,128)(2,1)} %broadcast_in_dim.62), calls=%async_computation | async-start | bytes 1179648 | tf_op jit(solution)/shard_map/all_to_all | solution.py:97
  39.3 12.3 %collective-permute-start.2 = (bf16[3,64,512]{2,1,0:T(8,128)(2,1)S(1)}, bf16[3,64,512]{2,1,0:T(8,128)(2,1)S(1)}, u32[]{:S(2)}, u32[]{:S(2)}) collective-permute-start(bf16[3,64,512]{2,1,0:T(8,128)(2,1)S(1)} %bitcast.135), channel_id=1, source_target_pairs={{0,8},{8,0},{1,9},{9,1},{2,10},{10,2},{3,11},{11,3},{4,12},{12,4},... | collective-permute-start | bytes 589832 | tf_op jit(solution)/shard_map/ppermute | solution.py:18
  51.7 0.7 copy-start.6
  53.2 10.8 %collective-permute-start.3 = (bf16[3,2,64,512]{3,2,1,0:T(8,128)(2,1)}, bf16[3,2,64,512]{3,2,1,0:T(8,128)(2,1)}, u32[]{:S(2)}, u32[]{:S(2)}) collective-permute-start(bf16[3,2,64,512]{3,2,1,0:T(8,128)(2,1)} %pad_maximum_fusion.3), channel_id=1, source_target_pairs={{0,16},{16,0},{32,48},{48,32},{1,17},{17,1},{33,49},{49,33},{2,18}... | collective-permute-start | bytes 1179656 | tf_op jit(solution)/shard_map/ppermute | solution.py:22
  56.3 16.3 %collective-permute-start.4 = (bf16[3,2,64,512]{3,2,1,0:T(8,128)(2,1)}, bf16[3,2,64,512]{3,2,1,0:T(8,128)(2,1)}, u32[]{:S(2)}, u32[]{:S(2)}) collective-permute-start(bf16[3,2,64,512]{3,2,1,0:T(8,128)(2,1)} %pad_maximum_fusion.3), channel_id=1, source_target_pairs={{0,32},{16,48},{32,0},{48,16},{1,33},{17,49},{33,1},{49,17},{2,34}... | collective-permute-start | bytes 1179656 | tf_op jit(solution)/shard_map/ppermute | solution.py:22
  60.7 20.0 %collective-permute-start.5 = (bf16[3,2,64,512]{3,2,1,0:T(8,128)(2,1)}, bf16[3,2,64,512]{3,2,1,0:T(8,128)(2,1)}, u32[]{:S(2)}, u32[]{:S(2)}) collective-permute-start(bf16[3,2,64,512]{3,2,1,0:T(8,128)(2,1)} %pad_maximum_fusion.3), channel_id=1, source_target_pairs={{0,48},{16,32},{32,16},{48,0},{1,49},{17,33},{33,17},{49,1},{2,50}... | collective-permute-start | bytes 1179656 | tf_op jit(solution)/shard_map/ppermute | solution.py:22
  67.0 16.0 %collective-permute-start.10 = (bf16[1024,256]{1,0:T(8,128)(2,1)}, bf16[1024,256]{1,0:T(8,128)(2,1)}, u32[]{:S(2)}, u32[]{:S(2)}) collective-permute-start(bf16[1024,256]{1,0:T(8,128)(2,1)} %bitcast.123), channel_id=1, source_target_pairs={{0,64},{64,0},{128,192},{192,128},{1,65},{65,1},{129,193},{193,129... | collective-permute-start | bytes 1572872 | tf_op jit(solution)/shard_map/ppermute | solution.py:22
  73.6 9.4 %copy-start.1 = (bf16[8,128,256]{2,1,0:T(8,128)(2,1)S(1)}, bf16[8,128,256]{2,1,0:T(8,128)(2,1)}, u32[]{:S(2)}) copy-start(bf16[8,128,256]{2,1,0:T(8,128)(2,1)} %copy.42) | copy-start | bytes 1572868
  73.7 10.5 %collective-permute-start.1 = (bf16[4,144,512]{2,1,0:T(8,128)(2,1)S(1)}, bf16[4,144,512]{2,1,0:T(8,128)(2,1)S(1)}, u32[]{:S(2)}, u32[]{:S(2)}) collective-permute-start(bf16[4,144,512]{2,1,0:T(8,128)(2,1)S(1)} %all-to-all-done), channel_id=1, source_target_pairs={{0,1},{1,0},{2,3},{3,2},{4,5},{5,4},{6,7},{7,6},{8,9},{9,8},{10,11... | collective-permute-start | bytes 1769480 | tf_op jit(solution)/shard_map/ppermute | solution.py:18
  88.5 4.5 %copy-start.5 = (bf16[1,2,2,2,64,512]{5,4,3,2,1,0:T(8,128)(2,1)S(1)}, bf16[1,2,2,2,64,512]{5,4,3,2,1,0:T(8,128)(2,1)}, u32[]{:S(2)}) copy-start(bf16[1,2,2,2,64,512]{5,4,3,2,1,0:T(8,128)(2,1)} %get-tuple-element.19) | copy-start | bytes 1572868
  88.5 48.5 %all-to-all-start.3 = ((bf16[4,400,512]{2,1,0:T(8,128)(2,1)}), bf16[4,400,512]{2,1,0:T(8,128)(2,1)}, u32[]{:S(2)}, u32[]{:S(2)}) async-start(bf16[4,400,512]{2,1,0:T(8,128)(2,1)} %pad_maximum_fusion), calls=%async_computation.3 | async-start | bytes 3276800 | tf_op jit(solution)/shard_map/all_to_all | solution.py:137
  93.0 1.0 copy-start.4
  93.8 1.1 copy-start.3
  95.7 9.6 %collective-permute-start.6 = (bf16[128,1024]{1,0:T(8,128)(2,1)S(1)}, bf16[128,1024]{1,0:T(8,128)(2,1)S(1)}, u32[]{:S(2)}, u32[]{:S(2)}) collective-permute-start(bf16[128,1024]{1,0:T(8,128)(2,1)S(1)} %get-tuple-element.24), channel_id=1, source_target_pairs={{0,64},{64,0},{128,192},{192,128},{1,65},{65,1},{129,193},{193,129... | collective-permute-start | bytes 786440 | tf_op jit(solution)/shard_map/ppermute | solution.py:22
  97.9 11.9 %collective-permute-start.7 = (bf16[128,1024]{1,0:T(8,128)(2,1)S(1)}, bf16[128,1024]{1,0:T(8,128)(2,1)S(1)}, u32[]{:S(2)}, u32[]{:S(2)}) collective-permute-start(bf16[128,1024]{1,0:T(8,128)(2,1)S(1)} %get-tuple-element.26), channel_id=1, source_target_pairs={{0,128},{64,192},{128,0},{192,64},{1,129},{65,193},{129,1},{193,65... | collective-permute-start | bytes 786440 | tf_op jit(solution)/shard_map/ppermute | solution.py:22
  100.8 15.1 %collective-permute-start.8 = (bf16[128,1024]{1,0:T(8,128)(2,1)S(1)}, bf16[128,1024]{1,0:T(8,128)(2,1)}, u32[]{:S(2)}, u32[]{:S(2)}) collective-permute-start(bf16[128,1024]{1,0:T(8,128)(2,1)S(1)} %get-tuple-element.25), channel_id=1, source_target_pairs={{0,192},{64,128},{128,64},{192,0},{1,193},{65,129},{129,65},{193,1... | collective-permute-start | bytes 786440 | tf_op jit(solution)/shard_map/ppermute | solution.py:22
  117.0 19.2 %collective-permute-start.9 = (bf16[64,1024]{1,0:T(8,128)(2,1)S(1)}, bf16[64,1024]{1,0:T(8,128)(2,1)S(1)}, u32[]{:S(2)}, u32[]{:S(2)}) collective-permute-start(bf16[64,1024]{1,0:T(8,128)(2,1)S(1)} %select_convert_fusion.1), channel_id=1, source_target_pairs={{0,256},{256,0},{1,257},{257,1},{2,258},{258,2},{3,259},{259,3},{4... | collective-permute-start | bytes 393224 | tf_op jit(solution)/shard_map/ppermute | solution.py:18
  137.0 29.6 %all-to-all-start.1 = ((bf16[8,64,128]{2,1,0:T(8,128)(2,1)}), bf16[8,64,128]{2,1,0:T(8,128)(2,1)S(1)}, u32[]{:S(2)}, u32[]{:S(2)}) async-start(bf16[8,64,128]{2,1,0:T(8,128)(2,1)} %copy.39), calls=%async_computation.1 | async-start | bytes 262144 | tf_op jit(solution)/shard_map/all_to_all | solution.py:123
  162.7 26.3 %collective-permute-start.11 = (bf16[208,512]{1,0:T(8,128)(2,1)S(1)}, bf16[208,512]{1,0:T(8,128)(2,1)S(1)}, u32[]{:S(2)}, u32[]{:S(2)}) collective-permute-start(bf16[208,512]{1,0:T(8,128)(2,1)S(1)} %pad_maximum_fusion.7), channel_id=1, source_target_pairs={{0,8},{8,0},{1,9},{9,1},{2,10},{10,2},{3,11},{11,3},{4,12},{12,4},... | collective-permute-start | bytes 638984 | tf_op jit(solution)/shard_map/ppermute | solution.py:18

commit v4 on v2

--- a/solution.py
+++ b/solution.py
@@ -44,7 +44,7 @@
     width = cols * lax.axis_size(DP)
     xs, ys = lax.axis_size("x"), lax.axis_size("y")
     members = lax.axis_size(GROUP)
-    x, y, zh, zl, c, zi = (lax.axis_index(a) for a in ("x", "y", "zh", "zl", "c", "zi"))
+    x, y, zh, c, zi = (lax.axis_index(a) for a in ("x", "y", "zh", "c", "zi"))
     blocks = feats // (members * rows)
 
     feature_rows = lax.dynamic_slice_in_dim(context, (y & 1) * (feats // 2), feats // 2, 1)
@@ -93,12 +93,10 @@
         [grad_proj, two_terms(gain_terms), mod_row, jnp.zeros((spare, cols), BF16)], axis=0
     )
     line = lax.axis_size("zl")
-    near = jnp.zeros((line, *packet.shape), BF16)
-    for k in range(line):
-        piece = packet if k == 0 else crossed(packet, "zl", k)
-        near = lax.dynamic_update_index_in_dim(near, piece, zl ^ k, 0)
-    others = swap(near, "c")
-    packets = in_order(c, near, others, 1).reshape(members, tok + 16, cols)
+    packets = jnp.broadcast_to(packet[None], (line, *packet.shape))
+    packets = lax.all_to_all(packets, "zl", 0, 0, tiled=True)
+    others = swap(packets, "c")
+    packets = in_order(c, packets, others, 1).reshape(members, tok + 16, cols)
     grads = packets[:, :tok].reshape(members * tok, cols)
     gain_part = jnp.sum(joined_terms(packets[:, tok:], towers), axis=0)
     ids = packets[:, tok + 2 * towers, :tok].astype(jnp.int32).reshape(members * tok)

time: 196 us -> 178 us (0.908)
  waiting for transfers between devices: 79.6 us -> 23.1 us
  starting transfers between devices: 86 us -> 121 us
  local copies, waits for them, and re-layouts: 5.83 us -> 12.1 us
  blocking collectives: 8.27 us -> 5.25 us
    ppermute x10 -> x7, waiting for transfers between devices: 34.5 us -> 7.41 us  [crossed(): lax.ppermute(value, axis, [(i, i ^ k) for i in range(lax.axis_size(axis))])]
    ppermute x5, waiting for transfers between devices: 35 us -> 11.3 us  [swap(): return lax.ppermute(value, axis, [(0, 1), (1, 0)])]
    all_to_all x1, starting transfers between devices: 8.2 us -> 28.5 us  [local(): settled = lax.all_to_all(total, GROUP, 0, 0, tiled=True)]
    ppermute x5, starting transfers between devices: 34.2 us -> 52.2 us  [swap(): return lax.ppermute(value, axis, [(0, 1), (1, 0)])]
    ppermute x10 -> x7, starting transfers between devices: 32.1 us -> 20.5 us  [crossed(): lax.ppermute(value, axis, [(i, i ^ k) for i in range(lax.axis_size(axis))])]
    all_to_all x1, waiting for transfers between devices: 10.1 us -> 0.01 us  [local(): partial = lax.all_to_all(partial, 'y', 0, 0, tiled=True)]
    all_to_all x0 -> x1, starting transfers between devices: none -> 4.75 us  [local(): packets = lax.all_to_all(packets, 'zl', 0, 0, tiled=True)]
    all_to_all x1, waiting for transfers between devices: 0.01 us -> 4.34 us  [local(): settled = lax.all_to_all(total, GROUP, 0, 0, tiled=True)]
  transfers between devices with their start and end apart: 18 -> 16, of which waited for: 8 -> 7; matrix products, arithmetic and copies ran while one was open for 7% -> 9% of each run, Pallas kernels for 0% -> 0%
where the time goes in v4:
time: 178 us; the launch traced here: 177 us
  starting transfers between devices  121 us (68%)
  waiting for transfers between devices  23.1 us (13%)
  local copies, waits for them, and re-layouts  12.1 us (7%)
  other arithmetic  8.06 us (5%)
  matrix products  6.58 us (4%)
  blocking collectives  5.25 us (3%)
    ppermute x5, starting transfers between devices, swap(): return lax.ppermute(value, axis, [(0, 1), (1, 0)])  52.2 us
    all_to_all x1, starting transfers between devices, local(): settled = lax.all_to_all(total, GROUP, 0, 0, tiled=True)  28.5 us
    ppermute x7, starting transfers between devices, crossed(): lax.ppermute(value, axis, [(i, i ^ k) for i in range(lax.axis_size(axis))])  20.5 us
    ppermute x5, waiting for transfers between devices, swap(): return lax.ppermute(value, axis, [(0, 1), (1, 0)])  11.3 us
    all_to_all x1, starting transfers between devices, local(): half = lax.all_to_all(feature_rows, GROUP, 0, 0, tiled=True)  10.4 us
    ppermute x7, waiting for transfers between devices, crossed(): lax.ppermute(value, axis, [(i, i ^ k) for i in range(lax.axis_size(axis))])  7.41 us
    all_gather x1, blocking collectives, local(): stats = lax.all_gather(stats, 'y')  5.25 us
    all_to_all x1, starting transfers between devices, local(): packets = lax.all_to_all(packets, 'zl', 0, 0, tiled=True)  4.75 us
  transfers between devices with their start and end apart: 16, of which 7 were waited for; matrix products, arithmetic and copies ran while one was open for 9% of the time, Pallas kernels for 0%

profile of v4, /device:TPU:1, one launch (start us, length us, event | category | flops | bytes accessed | tf_op | source)
XLA Modules:
  0.0 176.9 jit_solution(13755412131644085932)
XLA Ops:
  0.7 1.2 copy-done
  2.2 0.8 copy.41
  3.0 10.4 %all-to-all-start.3 = ((bf16[8,128,256]{1,2,0:T(8,128)(2,1)}), bf16[8,128,256]{1,2,0:T(8,128)(2,1)S(1)}, u32[]{:S(2)}, u32[]{:S(2)}) async-start(bf16[8,128,256]{1,2,0:T(8,128)(2,1)} %bitcast.30), calls=%async_computation.3 | async-start | bytes 1048576 | tf_op jit(solution)/shard_map/all_to_all | solution.py:53
  13.8 5.3 %all-gather.1 = f32[4,2,128]{2,1,0:T(2,128)S(1)} all-gather(f32[1,2,128]{2,1,0:T(2,128)S(1)} %maximum_bitcast_fusion), channel_id=2, replica_groups=mesh['zi'=2,'y'=4,'x'=4,'zh'=2,'zl'=4,'c'=2] {'y'}, dimensions={0}, use_global_device_ids=true | all-gather | bytes 5120 | tf_op jit(solution)/shard_map/all_gather | solution.py:80
  19.1 12.8 %collective-permute-start = (f32[2,128]{1,0:T(2,128)S(1)}, f32[2,128]{1,0:T(2,128)S(1)}, u32[]{:S(2)}, u32[]{:S(2)}) collective-permute-start(f32[2,128]{1,0:T(2,128)S(1)} %reduce_sum.47), channel_id=1, source_target_pairs={{0,256},{256,0},{1,257},{257,1},{2,258},{258,2},{3,259},{259,3},{4... | collective-permute-start | bytes 3080 | tf_op jit(solution)/shard_map/ppermute | solution.py:18
  32.0 0.9 collective-permute-done
  33.6 0.9 broadcast_in_dim.62
  34.6 4.8 %all-to-all-start = ((bf16[4,144,512]{2,1,0:T(8,128)(2,1)}), bf16[4,144,512]{2,1,0:T(8,128)(2,1)S(1)}, u32[]{:S(2)}, u32[]{:S(2)}) async-start(bf16[4,144,512]{2,1,0:T(8,128)(2,1)} %broadcast_in_dim.62), calls=%async_computation | async-start | bytes 1179648 | tf_op jit(solution)/shard_map/all_to_all | solution.py:97
  39.3 7.9 %collective-permute-start.2 = (bf16[3,64,512]{2,1,0:T(8,128)(2,1)S(1)}, bf16[3,64,512]{2,1,0:T(8,128)(2,1)S(1)}, u32[]{:S(2)}, u32[]{:S(2)}) collective-permute-start(bf16[3,64,512]{2,1,0:T(8,128)(2,1)S(1)} %bitcast.134), channel_id=1, source_target_pairs={{0,8},{8,0},{1,9},{9,1},{2,10},{10,2},{3,11},{11,3},{4,12},{12,4},... | collective-permute-start | bytes 589832 | tf_op jit(solution)/shard_map/ppermute | solution.py:18
  47.2 4.4 %collective-permute-done.2 = bf16[3,64,512]{2,1,0:T(8,128)(2,1)S(1)} collective-permute-done((bf16[3,64,512]{2,1,0:T(8,128)(2,1)S(1)}, bf16[3,64,512]{2,1,0:T(8,128)(2,1)S(1)}, u32[]{:S(2)}, u32[]{:S(2)}) %collective-permute-start.2) | collective-permute-done | bytes 196640 | tf_op jit(solution)/shard_map/ppermute | solution.py:18
  51.7 0.7 copy-done.3
  52.4 0.8 pad_maximum_fusion.3
  53.2 3.1 %collective-permute-start.3 = (bf16[3,2,64,512]{3,2,1,0:T(8,128)(2,1)}, bf16[3,2,64,512]{3,2,1,0:T(8,128)(2,1)}, u32[]{:S(2)}, u32[]{:S(2)}) collective-permute-start(bf16[3,2,64,512]{3,2,1,0:T(8,128)(2,1)} %pad_maximum_fusion.3), channel_id=1, source_target_pairs={{0,16},{16,0},{32,48},{48,32},{1,17},{17,1},{33,49},{49,33},{2,18}... | collective-permute-start | bytes 1179656 | tf_op jit(solution)/shard_map/ppermute | solution.py:22
  56.3 4.4 %collective-permute-start.4 = (bf16[3,2,64,512]{3,2,1,0:T(8,128)(2,1)}, bf16[3,2,64,512]{3,2,1,0:T(8,128)(2,1)}, u32[]{:S(2)}, u32[]{:S(2)}) collective-permute-start(bf16[3,2,64,512]{3,2,1,0:T(8,128)(2,1)} %pad_maximum_fusion.3), channel_id=1, source_target_pairs={{0,32},{16,48},{32,0},{48,16},{1,33},{17,49},{33,1},{49,17},{2,34}... | collective-permute-start | bytes 1179656 | tf_op jit(solution)/shard_map/ppermute | solution.py:22
  60.7 2.1 %collective-permute-start.5 = (bf16[3,2,64,512]{3,2,1,0:T(8,128)(2,1)}, bf16[3,2,64,512]{3,2,1,0:T(8,128)(2,1)}, u32[]{:S(2)}, u32[]{:S(2)}) collective-permute-start(bf16[3,2,64,512]{3,2,1,0:T(8,128)(2,1)} %pad_maximum_fusion.3), channel_id=1, source_target_pairs={{0,48},{16,32},{32,16},{48,0},{1,49},{17,33},{33,17},{49,1},{2,50}... | collective-permute-start | bytes 1179656 | tf_op jit(solution)/shard_map/ppermute | solution.py:22
  63.0 1.0 bitcast_dynamic-update-slice_fusion.2
  64.0 1.0 bitcast_dynamic-update-slice_fusion.1
  65.0 2.0 %copy.42 = bf16[8,128,256]{2,1,0:T(8,128)(2,1)} copy(bf16[8,128,256]{1,2,0:T(8,128)(2,1)} %copy-done.2) | data formatting | bytes 1048576 | tf_op jit(solution)/shard_map/all_to_all | solution.py:53
  67.1 1.9 %collective-permute-start.7 = (bf16[1024,256]{1,0:T(8,128)(2,1)}, bf16[1024,256]{1,0:T(8,128)(2,1)}, u32[]{:S(2)}, u32[]{:S(2)}) collective-permute-start(bf16[1024,256]{1,0:T(8,128)(2,1)} %bitcast.122), channel_id=1, source_target_pairs={{0,64},{64,0},{128,192},{192,128},{1,65},{65,1},{129,193},{193,129... | collective-permute-start | bytes 1572872 | tf_op jit(solution)/shard_map/ppermute | solution.py:22
  69.0 3.6 %collective-permute-done.4 = bf16[3,2,64,512]{3,2,1,0:T(8,128)(2,1)} collective-permute-done((bf16[3,2,64,512]{3,2,1,0:T(8,128)(2,1)}, bf16[3,2,64,512]{3,2,1,0:T(8,128)(2,1)}, u32[]{:S(2)}, u32[]{:S(2)}) %collective-permute-start.4) | collective-permute-done | bytes 393248 | tf_op jit(solution)/shard_map/ppermute | solution.py:22
  72.6 1.0 bitcast_dynamic-update-slice_fusion
  73.7 7.1 %collective-permute-start.1 = (bf16[4,144,512]{2,1,0:T(8,128)(2,1)S(1)}, bf16[4,144,512]{2,1,0:T(8,128)(2,1)S(1)}, u32[]{:S(2)}, u32[]{:S(2)}) collective-permute-start(bf16[4,144,512]{2,1,0:T(8,128)(2,1)S(1)} %all-to-all-done), channel_id=1, source_target_pairs={{0,1},{1,0},{2,3},{3,2},{4,5},{5,4},{6,7},{7,6},{8,9},{9,8},{10,11... | collective-permute-start | bytes 1769480 | tf_op jit(solution)/shard_map/ppermute | solution.py:18
  80.7 1.0 bitcast_dynamic-update-slice_fusion.3
  81.9 1.1 broadcast_select_fusion.1
  83.5 0.9 convolution_convert_fusion
  84.4 0.9 convolution_convert_fusion.1
  85.2 0.8 convolution_convert_fusion.2
  86.3 0.8 dynamic-slice_bitcast_fusion.2
  87.1 1.9 %collective-permute-start.8 = (bf16[400,512]{1,0:T(8,128)(2,1)}, bf16[400,512]{1,0:T(8,128)(2,1)}, u32[]{:S(2)}, u32[]{:S(2)}) collective-permute-start(bf16[400,512]{1,0:T(8,128)(2,1)} %get-tuple-element.17), channel_id=1, source_target_pairs={{0,16},{16,0},{32,48},{48,32},{1,17},{17,1},{33,49},{49,33},{2,18}... | collective-permute-start | bytes 1228808 | tf_op jit(solution)/shard_map/ppermute | solution.py:22
  89.0 3.4 %collective-permute-start.10 = (bf16[400,512]{1,0:T(8,128)(2,1)S(1)}, bf16[400,512]{1,0:T(8,128)(2,1)}, u32[]{:S(2)}, u32[]{:S(2)}) collective-permute-start(bf16[400,512]{1,0:T(8,128)(2,1)S(1)} %get-tuple-element.18), channel_id=1, source_target_pairs={{0,48},{16,32},{32,16},{48,0},{1,49},{17,33},{33,17},{49,1},{2,50}... | collective-permute-start | bytes 1228808 | tf_op jit(solution)/shard_map/ppermute | solution.py:22
  92.5 3.6 %collective-permute-start.9 = (bf16[400,512]{1,0:T(8,128)(2,1)S(1)}, bf16[400,512]{1,0:T(8,128)(2,1)}, u32[]{:S(2)}, u32[]{:S(2)}) collective-permute-start(bf16[400,512]{1,0:T(8,128)(2,1)S(1)} %get-tuple-element.19), channel_id=1, source_target_pairs={{0,32},{16,48},{32,0},{48,16},{1,33},{17,49},{33,1},{49,17},{2,34}... | collective-permute-start | bytes 1228808 | tf_op jit(solution)/shard_map/ppermute | solution.py:22
  96.1 0.7 fusion.43
  96.9 0.7 fusion.42
  97.6 1.8 %add_convert_fusion = bf16[512,1024]{1,0:T(8,128)(2,1)} fusion(f32[512,1024]{1,0:T(8,128)S(1)} %fusion.43, f32[512,1024]{1,0:T(8,128)S(1)} %fusion.42, bf16[512,512]{1,0:T(8,128)(2,1)S(1)} %bitcast.123, bf16[1024,512]{1,0:T(8,128)(2,1)S(1)} %bitcast.115, f32[1024]{0:T(1024)S(1)} %get-tuple-element.38, f32[1024]{0:T(1024)S(1)} %get-tuple-element.39, ...), kind=kOutput, calls=%fused_computation.1 | convolution fusion | flops 540016640 | bytes 6828032 | tf_op jit(solution)/shard_map/dot_general | solution.py:106
  99.4 4.2 %all-to-all-start.1 = ((bf16[4,128,1024]{2,1,0:T(8,128)(2,1)}), bf16[4,128,1024]{2,1,0:T(8,128)(2,1)}, u32[]{:S(2)}, u32[]{:S(2)}) async-start(bf16[4,128,1024]{2,1,0:T(8,128)(2,1)} %bitcast.121), calls=%async_computation.1 | async-start | bytes 2097152 | tf_op jit(solution)/shard_map/all_to_all | solution.py:111
  103.7 3.8 %collective-permute-done.9 = bf16[400,512]{1,0:T(8,128)(2,1)} collective-permute-done((bf16[400,512]{1,0:T(8,128)(2,1)S(1)}, bf16[400,512]{1,0:T(8,128)(2,1)}, u32[]{:S(2)}, u32[]{:S(2)}) %collective-permute-start.9) | collective-permute-done | bytes 409632 | tf_op jit(solution)/shard_map/ppermute | solution.py:22
  107.5 1.4 fusion.6
  109.1 7.0 %collective-permute-start.11 = (bf16[208,512]{1,0:T(8,128)(2,1)S(1)}, bf16[208,512]{1,0:T(8,128)(2,1)S(1)}, u32[]{:S(2)}, u32[]{:S(2)}) collective-permute-start(bf16[208,512]{1,0:T(8,128)(2,1)S(1)} %pad_maximum_fusion.7), channel_id=1, source_target_pairs={{0,8},{8,0},{1,9},{9,1},{2,10},{10,2},{3,11},{11,3},{4,12},{12,4},... | collective-permute-start | bytes 638984 | tf_op jit(solution)/shard_map/ppermute | solution.py:18
  116.1 3.4 %collective-permute-done.11 = bf16[208,512]{1,0:T(8,128)(2,1)S(1)} collective-permute-done((bf16[208,512]{1,0:T(8,128)(2,1)S(1)}, bf16[208,512]{1,0:T(8,128)(2,1)S(1)}, u32[]{:S(2)}, u32[]{:S(2)}) %collective-permute-start.11) | collective-permute-done | bytes 213024 | tf_op jit(solution)/shard_map/ppermute | solution.py:18
  119.6 1.5 convert_reduce_fusion
  121.1 17.4 %collective-permute-start.6 = (bf16[64,1024]{1,0:T(8,128)(2,1)S(1)}, bf16[64,1024]{1,0:T(8,128)(2,1)S(1)}, u32[]{:S(2)}, u32[]{:S(2)}) collective-permute-start(bf16[64,1024]{1,0:T(8,128)(2,1)S(1)} %select_convert_fusion.1), channel_id=1, source_target_pairs={{0,256},{256,0},{1,257},{257,1},{2,258},{258,2},{3,259},{259,3},{4... | collective-permute-start | bytes 393224 | tf_op jit(solution)/shard_map/ppermute | solution.py:18
  138.6 2.5 %collective-permute-done.6 = bf16[64,1024]{1,0:T(8,128)(2,1)S(1)} collective-permute-done((bf16[64,1024]{1,0:T(8,128)(2,1)S(1)}, bf16[64,1024]{1,0:T(8,128)(2,1)S(1)}, u32[]{:S(2)}, u32[]{:S(2)}) %collective-permute-start.6) | collective-permute-done | bytes 131104 | tf_op jit(solution)/shard_map/ppermute | solution.py:18
  141.2 0.7 copy.39
  141.9 28.5 %all-to-all-start.2 = ((bf16[8,64,128]{2,1,0:T(8,128)(2,1)}), bf16[8,64,128]{2,1,0:T(8,128)(2,1)S(1)}, u32[]{:S(2)}, u32[]{:S(2)}) async-start(bf16[8,64,128]{2,1,0:T(8,128)(2,1)} %copy.39), calls=%async_computation.2 | async-start | bytes 262144 | tf_op jit(solution)/shard_map/all_to_all | solution.py:118
  170.3 0.6 fusion.32
  170.9 0.8 fusion.10
  171.8 4.3 %all-to-all-done.2 = bf16[8,64,128]{2,1,0:T(8,128)(2,1)S(1)} async-done(((bf16[8,64,128]{2,1,0:T(8,128)(2,1)}), bf16[8,64,128]{2,1,0:T(8,128)(2,1)S(1)}, u32[]{:S(2)}, u32[]{:S(2)}) %all-to-all-start.2) | async-done | bytes 131104 | tf_op jit(solution)/shard_map/all_to_all | solution.py:118
  176.1 0.8 copy.45
  (65 shorter events, 2.7 us)
Async XLA Ops:
  0.6 1.2 copy-start
  1.9 11.5 %copy-start.4 = (bf16[128,512]{1,0:T(8,128)(2,1)S(1)}, bf16[128,512]{1,0:T(8,128)(2,1)}, u32[]{:S(2)}) copy-start(bf16[128,512]{1,0:T(8,128)(2,1)} %param.7) | copy-start | bytes 393220
  1.9 11.5 %copy-start.6 = (bf16[128,512]{1,0:T(8,128)(2,1)S(1)}, bf16[128,512]{1,0:T(8,128)(2,1)}, u32[]{:S(2)}) copy-start(bf16[128,512]{1,0:T(8,128)(2,1)} %param.8) | copy-start | bytes 393220
  1.9 11.5 %copy-start.7 = (f32[3,512]{1,0:T(4,128)S(1)}, f32[3,512]{1,0:T(4,128)}, u32[]{:S(2)}) copy-start(f32[3,512]{1,0:T(4,128)} %param.11) | copy-start | bytes 18436
  1.9 11.6 %copy-start.8 = (s32[128]{0:T(128)S(1)}, s32[128]{0:T(128)}, u32[]{:S(2)}) copy-start(s32[128]{0:T(128)} %param.9) | copy-start | bytes 1540
  3.0 36.3 %copy-start.5 = (bf16[64,3,512]{2,0,1:T(8,128)(2,1)S(1)}, bf16[64,3,512]{2,0,1:T(8,128)(2,1)}, u32[]{:S(2)}) copy-start(bf16[64,3,512]{2,0,1:T(8,128)(2,1)} %param.10) | copy-start | bytes 589828
  3.0 30.5 %all-to-all-start.3 = ((bf16[8,128,256]{1,2,0:T(8,128)(2,1)}), bf16[8,128,256]{1,2,0:T(8,128)(2,1)S(1)}, u32[]{:S(2)}, u32[]{:S(2)}) async-start(bf16[8,128,256]{1,2,0:T(8,128)(2,1)} %bitcast.30), calls=%async_computation.3 | async-start | bytes 1048576 | tf_op jit(solution)/shard_map/all_to_all | solution.py:53
  19.1 13.8 %collective-permute-start = (f32[2,128]{1,0:T(2,128)S(1)}, f32[2,128]{1,0:T(2,128)S(1)}, u32[]{:S(2)}, u32[]{:S(2)}) collective-permute-start(f32[2,128]{1,0:T(2,128)S(1)} %reduce_sum.47), channel_id=1, source_target_pairs={{0,256},{256,0},{1,257},{257,1},{2,258},{258,2},{3,259},{259,3},{4... | collective-permute-start | bytes 3080 | tf_op jit(solution)/shard_map/ppermute | solution.py:18
  33.6 1.0 copy-start.2
  34.6 39.1 %all-to-all-start = ((bf16[4,144,512]{2,1,0:T(8,128)(2,1)}), bf16[4,144,512]{2,1,0:T(8,128)(2,1)S(1)}, u32[]{:S(2)}, u32[]{:S(2)}) async-start(bf16[4,144,512]{2,1,0:T(8,128)(2,1)} %broadcast_in_dim.62), calls=%async_computation | async-start | bytes 1179648 | tf_op jit(solution)/shard_map/all_to_all | solution.py:97
  39.3 12.3 %collective-permute-start.2 = (bf16[3,64,512]{2,1,0:T(8,128)(2,1)S(1)}, bf16[3,64,512]{2,1,0:T(8,128)(2,1)S(1)}, u32[]{:S(2)}, u32[]{:S(2)}) collective-permute-start(bf16[3,64,512]{2,1,0:T(8,128)(2,1)S(1)} %bitcast.134), channel_id=1, source_target_pairs={{0,8},{8,0},{1,9},{9,1},{2,10},{10,2},{3,11},{11,3},{4,12},{12,4},... | collective-permute-start | bytes 589832 | tf_op jit(solution)/shard_map/ppermute | solution.py:18
  51.7 0.7 copy-start.3
  53.2 10.8 %collective-permute-start.3 = (bf16[3,2,64,512]{3,2,1,0:T(8,128)(2,1)}, bf16[3,2,64,512]{3,2,1,0:T(8,128)(2,1)}, u32[]{:S(2)}, u32[]{:S(2)}) collective-permute-start(bf16[3,2,64,512]{3,2,1,0:T(8,128)(2,1)} %pad_maximum_fusion.3), channel_id=1, source_target_pairs={{0,16},{16,0},{32,48},{48,32},{1,17},{17,1},{33,49},{49,33},{2,18}... | collective-permute-start | bytes 1179656 | tf_op jit(solution)/shard_map/ppermute | solution.py:22
  56.3 16.3 %collective-permute-start.4 = (bf16[3,2,64,512]{3,2,1,0:T(8,128)(2,1)}, bf16[3,2,64,512]{3,2,1,0:T(8,128)(2,1)}, u32[]{:S(2)}, u32[]{:S(2)}) collective-permute-start(bf16[3,2,64,512]{3,2,1,0:T(8,128)(2,1)} %pad_maximum_fusion.3), channel_id=1, source_target_pairs={{0,32},{16,48},{32,0},{48,16},{1,33},{17,49},{33,1},{49,17},{2,34}... | collective-permute-start | bytes 1179656 | tf_op jit(solution)/shard_map/ppermute | solution.py:22
  60.7 20.0 %collective-permute-start.5 = (bf16[3,2,64,512]{3,2,1,0:T(8,128)(2,1)}, bf16[3,2,64,512]{3,2,1,0:T(8,128)(2,1)}, u32[]{:S(2)}, u32[]{:S(2)}) collective-permute-start(bf16[3,2,64,512]{3,2,1,0:T(8,128)(2,1)} %pad_maximum_fusion.3), channel_id=1, source_target_pairs={{0,48},{16,32},{32,16},{48,0},{1,49},{17,33},{33,17},{49,1},{2,50}... | collective-permute-start | bytes 1179656 | tf_op jit(solution)/shard_map/ppermute | solution.py:22
  67.1 14.9 %collective-permute-start.7 = (bf16[1024,256]{1,0:T(8,128)(2,1)}, bf16[1024,256]{1,0:T(8,128)(2,1)}, u32[]{:S(2)}, u32[]{:S(2)}) collective-permute-start(bf16[1024,256]{1,0:T(8,128)(2,1)} %bitcast.122), channel_id=1, source_target_pairs={{0,64},{64,0},{128,192},{192,128},{1,65},{65,1},{129,193},{193,129... | collective-permute-start | bytes 1572872 | tf_op jit(solution)/shard_map/ppermute | solution.py:22
  73.7 8.3 %copy-start.1 = (bf16[8,128,256]{2,1,0:T(8,128)(2,1)S(1)}, bf16[8,128,256]{2,1,0:T(8,128)(2,1)}, u32[]{:S(2)}) copy-start(bf16[8,128,256]{2,1,0:T(8,128)(2,1)} %copy.42) | copy-start | bytes 1572868
  73.7 9.4 %collective-permute-start.1 = (bf16[4,144,512]{2,1,0:T(8,128)(2,1)S(1)}, bf16[4,144,512]{2,1,0:T(8,128)(2,1)S(1)}, u32[]{:S(2)}, u32[]{:S(2)}) collective-permute-start(bf16[4,144,512]{2,1,0:T(8,128)(2,1)S(1)} %all-to-all-done), channel_id=1, source_target_pairs={{0,1},{1,0},{2,3},{3,2},{4,5},{5,4},{6,7},{7,6},{8,9},{9,8},{10,11... | collective-permute-start | bytes 1769480 | tf_op jit(solution)/shard_map/ppermute | solution.py:18
  87.1 16.6 %collective-permute-start.8 = (bf16[400,512]{1,0:T(8,128)(2,1)}, bf16[400,512]{1,0:T(8,128)(2,1)}, u32[]{:S(2)}, u32[]{:S(2)}) collective-permute-start(bf16[400,512]{1,0:T(8,128)(2,1)} %get-tuple-element.17), channel_id=1, source_target_pairs={{0,16},{16,0},{32,48},{48,32},{1,17},{17,1},{33,49},{49,33},{2,18}... | collective-permute-start | bytes 1228808 | tf_op jit(solution)/shard_map/ppermute | solution.py:22
  89.0 14.6 %collective-permute-start.10 = (bf16[400,512]{1,0:T(8,128)(2,1)S(1)}, bf16[400,512]{1,0:T(8,128)(2,1)}, u32[]{:S(2)}, u32[]{:S(2)}) collective-permute-start(bf16[400,512]{1,0:T(8,128)(2,1)S(1)} %get-tuple-element.18), channel_id=1, source_target_pairs={{0,48},{16,32},{32,16},{48,0},{1,49},{17,33},{33,17},{49,1},{2,50}... | collective-permute-start | bytes 1228808 | tf_op jit(solution)/shard_map/ppermute | solution.py:22
  92.5 15.0 %collective-permute-start.9 = (bf16[400,512]{1,0:T(8,128)(2,1)S(1)}, bf16[400,512]{1,0:T(8,128)(2,1)}, u32[]{:S(2)}, u32[]{:S(2)}) collective-permute-start(bf16[400,512]{1,0:T(8,128)(2,1)S(1)} %get-tuple-element.19), channel_id=1, source_target_pairs={{0,32},{16,48},{32,0},{48,16},{1,33},{17,49},{33,1},{49,17},{2,34}... | collective-permute-start | bytes 1228808 | tf_op jit(solution)/shard_map/ppermute | solution.py:22
  99.4 20.2 %all-to-all-start.1 = ((bf16[4,128,1024]{2,1,0:T(8,128)(2,1)}), bf16[4,128,1024]{2,1,0:T(8,128)(2,1)}, u32[]{:S(2)}, u32[]{:S(2)}) async-start(bf16[4,128,1024]{2,1,0:T(8,128)(2,1)} %bitcast.121), calls=%async_computation.1 | async-start | bytes 2097152 | tf_op jit(solution)/shard_map/all_to_all | solution.py:111
  109.1 10.5 %collective-permute-start.11 = (bf16[208,512]{1,0:T(8,128)(2,1)S(1)}, bf16[208,512]{1,0:T(8,128)(2,1)S(1)}, u32[]{:S(2)}, u32[]{:S(2)}) collective-permute-start(bf16[208,512]{1,0:T(8,128)(2,1)S(1)} %pad_maximum_fusion.7), channel_id=1, source_target_pairs={{0,8},{8,0},{1,9},{9,1},{2,10},{10,2},{3,11},{11,3},{4,12},{12,4},... | collective-permute-start | bytes 638984 | tf_op jit(solution)/shard_map/ppermute | solution.py:18
  121.1 20.0 %collective-permute-start.6 = (bf16[64,1024]{1,0:T(8,128)(2,1)S(1)}, bf16[64,1024]{1,0:T(8,128)(2,1)S(1)}, u32[]{:S(2)}, u32[]{:S(2)}) collective-permute-start(bf16[64,1024]{1,0:T(8,128)(2,1)S(1)} %select_convert_fusion.1), channel_id=1, source_target_pairs={{0,256},{256,0},{1,257},{257,1},{2,258},{258,2},{3,259},{259,3},{4... | collective-permute-start | bytes 393224 | tf_op jit(solution)/shard_map/ppermute | solution.py:18
  141.9 34.2 %all-to-all-start.2 = ((bf16[8,64,128]{2,1,0:T(8,128)(2,1)}), bf16[8,64,128]{2,1,0:T(8,128)(2,1)S(1)}, u32[]{:S(2)}, u32[]{:S(2)}) async-start(bf16[8,64,128]{2,1,0:T(8,128)(2,1)} %copy.39), calls=%async_computation.2 | async-start | bytes 262144 | tf_op jit(solution)/shard_map/all_to_all | solution.py:118

commit v5 on v4

--- a/solution.py
+++ b/solution.py
@@ -12,6 +12,7 @@
 EPS = 1e-06
 F32 = jnp.float32
 BF16 = jnp.bfloat16
+EXTRA = 8
 
 
 def swap(value, axis):
@@ -87,7 +88,7 @@
     gain_terms = jnp.dot(onehot.T, cot_float * normed, precision=lax.Precision.HIGHEST)
     grad_proj = (inverse_rms * (scaled - normed * (inner / width))).astype(BF16)
 
-    spare = 16 - 2 * towers - 1
+    spare = EXTRA - 2 * towers - 1
     mod_row = jnp.pad(modality.astype(BF16), (0, cols - tok))[None]
     packet = jnp.concatenate(
         [grad_proj, two_terms(gain_terms), mod_row, jnp.zeros((spare, cols), BF16)], axis=0
@@ -96,7 +97,7 @@
     packets = jnp.broadcast_to(packet[None], (line, *packet.shape))
     packets = lax.all_to_all(packets, "zl", 0, 0, tiled=True)
     others = swap(packets, "c")
-    packets = in_order(c, packets, others, 1).reshape(members, tok + 16, cols)
+    packets = in_order(c, packets, others, 1).reshape(members, tok + EXTRA, cols)
     grads = packets[:, :tok].reshape(members * tok, cols)
     gain_part = jnp.sum(joined_terms(packets[:, tok:], towers), axis=0)
     ids = packets[:, tok + 2 * towers, :tok].astype(jnp.int32).reshape(members * tok)
@@ -126,8 +127,8 @@
         )
         update = update.astype(BF16)
         updates.append(update.reshape(xs, 2 * rows, cols))
-    gain_rows = jnp.pad(two_terms(gain_part), ((0, 16 - 2 * towers), (0, 0)))
-    updates.append(jnp.broadcast_to(gain_rows[None], (xs, 16, cols)))
+    gain_rows = jnp.pad(two_terms(gain_part), ((0, EXTRA - 2 * towers), (0, 0)))
+    updates.append(jnp.broadcast_to(gain_rows[None], (xs, EXTRA, cols)))
     updates = jnp.concatenate(updates, axis=1)
     parts = []
     for k in range(xs):
@@ -140,7 +141,7 @@
     gain_part = joined_terms(total_part[size:], towers)
     kept = jnp.where(zh == 0, weight_part[:, 0], weight_part[:, 1])
     sent = jnp.where(zh == 0, weight_part[:, 1], weight_part[:, 0]).astype(BF16)
-    gain_rows = jnp.pad(two_terms(gain_part), ((0, 16 - 2 * towers), (0, 0)))
+    gain_rows = jnp.pad(two_terms(gain_part), ((0, EXTRA - 2 * towers), (0, 0)))
     sent = jnp.concatenate([sent.reshape(towers * rows, cols), gain_rows], axis=0)
     got = swap(sent, "zh")
     grad_weight = kept + got[: towers * rows].reshape(towers, rows, cols).astype(F32)

time: 178 us -> 197 us (1.11)
  waiting for transfers between devices: 23.1 us -> 74.9 us
  starting transfers between devices: 121 us -> 86.5 us
  local copies, waits for them, and re-layouts: 12.1 us -> 8.01 us
  blocking collectives: 5.25 us -> 8.79 us
  matrix products: 6.58 us -> 8.75 us
    all_to_all x1, starting transfers between devices: 28.5 us -> 4.09 us  [local(): settled = lax.all_to_all(total, GROUP, 0, 0, tiled=True)]
    ppermute x7, waiting for transfers between devices: 7.41 us -> 30.3 us  [crossed(): lax.ppermute(value, axis, [(i, i ^ k) for i in range(lax.axis_size(axis))])]
    ppermute x5, waiting for transfers between devices: 11.3 us -> 31.9 us  [swap(): return lax.ppermute(value, axis, [(0, 1), (1, 0)])]
    all_to_all x1, waiting for transfers between devices: 0.01 us -> 8.39 us  [local(): packets = lax.all_to_all(packets, 'zl', 0, 0, tiled=True)]
    ppermute x5, starting transfers between devices: 52.2 us -> 44.6 us  [swap(): return lax.ppermute(value, axis, [(0, 1), (1, 0)])]
    all_gather x1, blocking collectives: 5.25 us -> 8.79 us  [local(): stats = lax.all_gather(stats, 'y')]
    dynamic_update_slice x3, local copies, waits for them, and re-layouts: 3.09 us -> 1.08 us  [local(): lax.dynamic_update_slice(every, piece[:, None, :, None], (0, source & 1,...]
  transfers between devices with their start and end apart: 16 -> 16, of which waited for: 7 -> 10; matrix products, arithmetic and copies ran while one was open for 9% -> 6% of each run, Pallas kernels for 0% -> 0%
where the time goes in v5:
time: 197 us; the launch traced here: 196 us
  starting transfers between devices  86.5 us (44%)
  waiting for transfers between devices  74.9 us (38%)
  blocking collectives  8.79 us (4%)
  matrix products  8.75 us (4%)
  local copies, waits for them, and re-layouts  8.01 us (4%)
  other arithmetic  7.93 us (4%)
    ppermute x5, starting transfers between devices, swap(): return lax.ppermute(value, axis, [(0, 1), (1, 0)])  44.6 us
    ppermute x5, waiting for transfers between devices, swap(): return lax.ppermute(value, axis, [(0, 1), (1, 0)])  31.9 us
    ppermute x7, waiting for transfers between devices, crossed(): lax.ppermute(value, axis, [(i, i ^ k) for i in range(lax.axis_size(axis))])  30.3 us
    ppermute x7, starting transfers between devices, crossed(): lax.ppermute(value, axis, [(i, i ^ k) for i in range(lax.axis_size(axis))])  20.5 us
    all_to_all x1, starting transfers between devices, local(): half = lax.all_to_all(feature_rows, GROUP, 0, 0, tiled=True)  9.66 us
    all_gather x1, blocking collectives, local(): stats = lax.all_gather(stats, 'y')  8.79 us
    all_to_all x1, waiting for transfers between devices, local(): packets = lax.all_to_all(packets, 'zl', 0, 0, tiled=True)  8.39 us
    all_to_all x1, waiting for transfers between devices, local(): settled = lax.all_to_all(total, GROUP, 0, 0, tiled=True)  4.39 us
  transfers between devices with their start and end apart: 16, of which 10 were waited for; matrix products, arithmetic and copies ran while one was open for 6% of the time, Pallas kernels for 0%

profile of v5, /device:TPU:1, one launch (start us, length us, event | category | flops | bytes accessed | tf_op | source)
XLA Modules:
  0.0 196.1 jit_solution(5442665815413708938)
XLA Ops:
  0.7 1.5 fusion.16
  2.2 8.8 %all-gather.1 = f32[4,2,128]{2,1,0:T(2,128)S(1)} all-gather(f32[1,2,128]{2,1,0:T(2,128)S(1)} %maximum_bitcast_fusion), channel_id=2, replica_groups=mesh['zi'=2,'y'=4,'x'=4,'zh'=2,'zl'=4,'c'=2] {'y'}, dimensions={0}, use_global_device_ids=true | all-gather | bytes 5120 | tf_op jit(solution)/shard_map/all_gather | solution.py:81
  11.0 15.4 %collective-permute-start = (f32[2,128]{1,0:T(2,128)S(1)}, f32[2,128]{1,0:T(2,128)S(1)}, u32[]{:S(2)}, u32[]{:S(2)}) collective-permute-start(f32[2,128]{1,0:T(2,128)S(1)} %reduce_sum.47), channel_id=1, source_target_pairs={{0,256},{256,0},{1,257},{257,1},{2,258},{258,2},{3,259},{259,3},{4... | collective-permute-start | bytes 3080 | tf_op jit(solution)/shard_map/ppermute | solution.py:19
  26.4 0.7 convert_element_type.131
  27.4 1.3 fusion.27
  28.7 1.0 fusion.14
  29.8 0.8 broadcast_in_dim.62
  30.7 3.5 %all-to-all-start = ((bf16[4,136,512]{2,1,0:T(8,128)(2,1)}), bf16[4,136,512]{2,1,0:T(8,128)(2,1)S(1)}, u32[]{:S(2)}, u32[]{:S(2)}) async-start(bf16[4,136,512]{2,1,0:T(8,128)(2,1)} %broadcast_in_dim.62), calls=%async_computation | async-start | bytes 1114112 | tf_op jit(solution)/shard_map/all_to_all | solution.py:98
  34.1 7.6 %collective-permute-start.2 = (bf16[3,64,512]{2,1,0:T(8,128)(2,1)S(1)}, bf16[3,64,512]{2,1,0:T(8,128)(2,1)S(1)}, u32[]{:S(2)}, u32[]{:S(2)}) collective-permute-start(bf16[3,64,512]{2,1,0:T(8,128)(2,1)S(1)} %bitcast.134), channel_id=1, source_target_pairs={{0,8},{8,0},{1,9},{9,1},{2,10},{10,2},{3,11},{11,3},{4,12},{12,4},... | collective-permute-start | bytes 589832 | tf_op jit(solution)/shard_map/ppermute | solution.py:19
  42.1 0.9 copy.41
  42.9 8.4 %all-to-all-done = bf16[4,136,512]{2,1,0:T(8,128)(2,1)S(1)} async-done(((bf16[4,136,512]{2,1,0:T(8,128)(2,1)}), bf16[4,136,512]{2,1,0:T(8,128)(2,1)S(1)}, u32[]{:S(2)}, u32[]{:S(2)}) %all-to-all-start) | async-done | bytes 557088 | tf_op jit(solution)/shard_map/all_to_all | solution.py:98
  51.3 9.7 %all-to-all-start.3 = ((bf16[8,128,256]{1,2,0:T(8,128)(2,1)}), bf16[8,128,256]{1,2,0:T(8,128)(2,1)S(1)}, u32[]{:S(2)}, u32[]{:S(2)}) async-start(bf16[8,128,256]{1,2,0:T(8,128)(2,1)} %bitcast.30), calls=%async_computation.3 | async-start | bytes 1048576 | tf_op jit(solution)/shard_map/all_to_all | solution.py:54
  61.0 3.1 %collective-permute-start.3 = (bf16[3,2,64,512]{3,2,1,0:T(8,128)(2,1)S(1)}, bf16[3,2,64,512]{3,2,1,0:T(8,128)(2,1)}, u32[]{:S(2)}, u32[]{:S(2)}) collective-permute-start(bf16[3,2,64,512]{3,2,1,0:T(8,128)(2,1)S(1)} %pad_maximum_fusion.3), channel_id=1, source_target_pairs={{0,16},{16,0},{32,48},{48,32},{1,17},{17,1},{33,49},{49,33},{2,18}... | collective-permute-start | bytes 1179656 | tf_op jit(solution)/shard_map/ppermute | solution.py:23
  64.2 4.4 %collective-permute-start.4 = (bf16[3,2,64,512]{3,2,1,0:T(8,128)(2,1)S(1)}, bf16[3,2,64,512]{3,2,1,0:T(8,128)(2,1)S(1)}, u32[]{:S(2)}, u32[]{:S(2)}) collective-permute-start(bf16[3,2,64,512]{3,2,1,0:T(8,128)(2,1)S(1)} %pad_maximum_fusion.3), channel_id=1, source_target_pairs={{0,32},{16,48},{32,0},{48,16},{1,33},{17,49},{33,1},{49,17},{2,34}... | collective-permute-start | bytes 1179656 | tf_op jit(solution)/shard_map/ppermute | solution.py:23
  68.6 2.1 %collective-permute-start.5 = (bf16[3,2,64,512]{3,2,1,0:T(8,128)(2,1)S(1)}, bf16[3,2,64,512]{3,2,1,0:T(8,128)(2,1)S(1)}, u32[]{:S(2)}, u32[]{:S(2)}) collective-permute-start(bf16[3,2,64,512]{3,2,1,0:T(8,128)(2,1)S(1)} %pad_maximum_fusion.3), channel_id=1, source_target_pairs={{0,48},{16,32},{32,16},{48,0},{1,49},{17,33},{33,17},{49,1},{2,50}... | collective-permute-start | bytes 1179656 | tf_op jit(solution)/shard_map/ppermute | solution.py:23
  70.9 2.7 %collective-permute-done.3 = bf16[3,2,64,512]{3,2,1,0:T(8,128)(2,1)} collective-permute-done((bf16[3,2,64,512]{3,2,1,0:T(8,128)(2,1)S(1)}, bf16[3,2,64,512]{3,2,1,0:T(8,128)(2,1)}, u32[]{:S(2)}, u32[]{:S(2)}) %collective-permute-start.3) | collective-permute-done | bytes 393248 | tf_op jit(solution)/shard_map/ppermute | solution.py:23
  73.6 1.0 bitcast_dynamic-update-slice_fusion.1
  74.6 3.5 %collective-permute-start.1 = (bf16[4,136,512]{2,1,0:T(8,128)(2,1)S(1)}, bf16[4,136,512]{2,1,0:T(8,128)(2,1)}, u32[]{:S(2)}, u32[]{:S(2)}) collective-permute-start(bf16[4,136,512]{2,1,0:T(8,128)(2,1)S(1)} %all-to-all-done), channel_id=1, source_target_pairs={{0,1},{1,0},{2,3},{3,2},{4,5},{5,4},{6,7},{7,6},{8,9},{9,8},{10,11... | collective-permute-start | bytes 1671176 | tf_op jit(solution)/shard_map/ppermute | solution.py:19
  78.1 6.0 %collective-permute-done.4 = bf16[3,2,64,512]{3,2,1,0:T(8,128)(2,1)S(1)} collective-permute-done((bf16[3,2,64,512]{3,2,1,0:T(8,128)(2,1)S(1)}, bf16[3,2,64,512]{3,2,1,0:T(8,128)(2,1)S(1)}, u32[]{:S(2)}, u32[]{:S(2)}) %collective-permute-start.4) | collective-permute-done | bytes 393248 | tf_op jit(solution)/shard_map/ppermute | solution.py:23
  84.2 5.9 %collective-permute-done.5 = bf16[3,2,64,512]{3,2,1,0:T(8,128)(2,1)S(1)} collective-permute-done((bf16[3,2,64,512]{3,2,1,0:T(8,128)(2,1)S(1)}, bf16[3,2,64,512]{3,2,1,0:T(8,128)(2,1)S(1)}, u32[]{:S(2)}, u32[]{:S(2)}) %collective-permute-start.5) | collective-permute-done | bytes 393248 | tf_op jit(solution)/shard_map/ppermute | solution.py:23
  90.2 1.1 fusion.41
  91.5 1.9 collective-permute-start.7
  93.4 1.1 select_bitcast_fusion.1
  94.9 0.7 copy-done.2
  95.6 0.7 fusion.43
  96.4 0.7 fusion.42
  97.1 8.2 %collective-permute-done.7 = bf16[1024,256]{1,0:T(8,128)(2,1)S(1)} collective-permute-done((bf16[1024,256]{1,0:T(8,128)(2,1)S(1)}, bf16[1024,256]{1,0:T(8,128)(2,1)S(1)}, u32[]{:S(2)}, u32[]{:S(2)}) %collective-permute-start.7) | collective-permute-done | bytes 524320 | tf_op jit(solution)/shard_map/ppermute | solution.py:23
  105.4 0.9 convolution_convert_fusion
  106.3 0.9 convolution_convert_fusion.1
  107.2 0.9 convolution_convert_fusion.2
  108.1 1.1 dynamic-slice_bitcast_fusion.2
  109.2 1.9 collective-permute-start.8
  111.1 2.1 %collective-permute-start.10 = (bf16[392,512]{1,0:T(8,128)(2,1)}, bf16[392,512]{1,0:T(8,128)(2,1)}, u32[]{:S(2)}, u32[]{:S(2)}) collective-permute-start(bf16[392,512]{1,0:T(8,128)(2,1)} %get-tuple-element.18), channel_id=1, source_target_pairs={{0,48},{16,32},{32,16},{48,0},{1,49},{17,33},{33,17},{49,1},{2,50}... | collective-permute-start | bytes 1204232 | tf_op jit(solution)/shard_map/ppermute | solution.py:23
  113.3 5.0 %collective-permute-start.9 = (bf16[392,512]{1,0:T(8,128)(2,1)}, bf16[392,512]{1,0:T(8,128)(2,1)}, u32[]{:S(2)}, u32[]{:S(2)}) collective-permute-start(bf16[392,512]{1,0:T(8,128)(2,1)} %get-tuple-element.19), channel_id=1, source_target_pairs={{0,32},{16,48},{32,0},{48,16},{1,33},{17,49},{33,1},{49,17},{2,34}... | collective-permute-start | bytes 1204232 | tf_op jit(solution)/shard_map/ppermute | solution.py:23
  118.2 1.9 add_convert_fusion
  120.1 4.2 %all-to-all-start.1 = ((bf16[4,128,1024]{2,1,0:T(8,128)(2,1)}), bf16[4,128,1024]{2,1,0:T(8,128)(2,1)}, u32[]{:S(2)}, u32[]{:S(2)}) async-start(bf16[4,128,1024]{2,1,0:T(8,128)(2,1)} %bitcast.121), calls=%async_computation.1 | async-start | bytes 2097152 | tf_op jit(solution)/shard_map/all_to_all | solution.py:112
  124.4 7.4 %collective-permute-done.10 = bf16[392,512]{1,0:T(8,128)(2,1)} collective-permute-done((bf16[392,512]{1,0:T(8,128)(2,1)}, bf16[392,512]{1,0:T(8,128)(2,1)}, u32[]{:S(2)}, u32[]{:S(2)}) %collective-permute-start.10) | collective-permute-done | bytes 401440 | tf_op jit(solution)/shard_map/ppermute | solution.py:23
  131.8 1.4 fusion.6
  133.4 6.7 %collective-permute-start.11 = (bf16[200,512]{1,0:T(8,128)(2,1)S(1)}, bf16[200,512]{1,0:T(8,128)(2,1)S(1)}, u32[]{:S(2)}, u32[]{:S(2)}) collective-permute-start(bf16[200,512]{1,0:T(8,128)(2,1)S(1)} %pad_maximum_fusion.7), channel_id=1, source_target_pairs={{0,8},{8,0},{1,9},{9,1},{2,10},{10,2},{3,11},{11,3},{4,12},{12,4},... | collective-permute-start | bytes 614408 | tf_op jit(solution)/shard_map/ppermute | solution.py:19
  140.1 18.9 %collective-permute-done.11 = bf16[200,512]{1,0:T(8,128)(2,1)S(1)} collective-permute-done((bf16[200,512]{1,0:T(8,128)(2,1)S(1)}, bf16[200,512]{1,0:T(8,128)(2,1)S(1)}, u32[]{:S(2)}, u32[]{:S(2)}) %collective-permute-start.11) | collective-permute-done | bytes 204832 | tf_op jit(solution)/shard_map/ppermute | solution.py:19
  159.1 1.5 convert_reduce_fusion
  160.6 11.4 %collective-permute-start.6 = (bf16[64,1024]{1,0:T(8,128)(2,1)S(1)}, bf16[64,1024]{1,0:T(8,128)(2,1)S(1)}, u32[]{:S(2)}, u32[]{:S(2)}) collective-permute-start(bf16[64,1024]{1,0:T(8,128)(2,1)S(1)} %select_convert_fusion.1), channel_id=1, source_target_pairs={{0,256},{256,0},{1,257},{257,1},{2,258},{258,2},{3,259},{259,3},{4... | collective-permute-start | bytes 393224 | tf_op jit(solution)/shard_map/ppermute | solution.py:19
  172.0 12.7 %collective-permute-done.6 = bf16[64,1024]{1,0:T(8,128)(2,1)S(1)} collective-permute-done((bf16[64,1024]{1,0:T(8,128)(2,1)S(1)}, bf16[64,1024]{1,0:T(8,128)(2,1)S(1)}, u32[]{:S(2)}, u32[]{:S(2)}) %collective-permute-start.6) | collective-permute-done | bytes 131104 | tf_op jit(solution)/shard_map/ppermute | solution.py:19
  184.8 0.7 copy.39
  185.4 4.1 %all-to-all-start.2 = ((bf16[8,64,128]{2,1,0:T(8,128)(2,1)}), bf16[8,64,128]{2,1,0:T(8,128)(2,1)S(1)}, u32[]{:S(2)}, u32[]{:S(2)}) async-start(bf16[8,64,128]{2,1,0:T(8,128)(2,1)} %copy.39), calls=%async_computation.2 | async-start | bytes 262144 | tf_op jit(solution)/shard_map/all_to_all | solution.py:119
  190.1 0.8 fusion.10
  191.0 4.4 %all-to-all-done.2 = bf16[8,64,128]{2,1,0:T(8,128)(2,1)S(1)} async-done(((bf16[8,64,128]{2,1,0:T(8,128)(2,1)}), bf16[8,64,128]{2,1,0:T(8,128)(2,1)S(1)}, u32[]{:S(2)}, u32[]{:S(2)}) %all-to-all-start.2) | async-done | bytes 131104 | tf_op jit(solution)/shard_map/all_to_all | solution.py:119
  195.4 0.8 copy.45
  (55 shorter events, 2.7 us)
Async XLA Ops:
  0.6 41.1 %copy-start = (bf16[128,4096]{1,0:T(8,128)(2,1)S(1)}, bf16[128,4096]{1,0:T(8,128)(2,1)}, u32[]{:S(2)}) copy-start(bf16[128,4096]{1,0:T(8,128)(2,1)} %param.6) | copy-start | bytes 3145732
  0.6 33.5 %copy-start.3 = (bf16[64,3,512]{2,0,1:T(8,128)(2,1)S(1)}, bf16[64,3,512]{2,0,1:T(8,128)(2,1)}, u32[]{:S(2)}) copy-start(bf16[64,3,512]{2,0,1:T(8,128)(2,1)} %param.10) | copy-start | bytes 589828
  11.0 16.4 %collective-permute-start = (f32[2,128]{1,0:T(2,128)S(1)}, f32[2,128]{1,0:T(2,128)S(1)}, u32[]{:S(2)}, u32[]{:S(2)}) collective-permute-start(f32[2,128]{1,0:T(2,128)S(1)} %reduce_sum.47), channel_id=1, source_target_pairs={{0,256},{256,0},{1,257},{257,1},{2,258},{258,2},{3,259},{259,3},{4... | collective-permute-start | bytes 3080 | tf_op jit(solution)/shard_map/ppermute | solution.py:19
  30.7 20.7 %all-to-all-start = ((bf16[4,136,512]{2,1,0:T(8,128)(2,1)}), bf16[4,136,512]{2,1,0:T(8,128)(2,1)S(1)}, u32[]{:S(2)}, u32[]{:S(2)}) async-start(bf16[4,136,512]{2,1,0:T(8,128)(2,1)} %broadcast_in_dim.62), calls=%async_computation | async-start | bytes 1114112 | tf_op jit(solution)/shard_map/all_to_all | solution.py:98
  34.1 26.8 %collective-permute-start.2 = (bf16[3,64,512]{2,1,0:T(8,128)(2,1)S(1)}, bf16[3,64,512]{2,1,0:T(8,128)(2,1)S(1)}, u32[]{:S(2)}, u32[]{:S(2)}) collective-permute-start(bf16[3,64,512]{2,1,0:T(8,128)(2,1)S(1)} %bitcast.134), channel_id=1, source_target_pairs={{0,8},{8,0},{1,9},{9,1},{2,10},{10,2},{3,11},{11,3},{4,12},{12,4},... | collective-permute-start | bytes 589832 | tf_op jit(solution)/shard_map/ppermute | solution.py:19
  51.3 39.9 %all-to-all-start.3 = ((bf16[8,128,256]{1,2,0:T(8,128)(2,1)}), bf16[8,128,256]{1,2,0:T(8,128)(2,1)S(1)}, u32[]{:S(2)}, u32[]{:S(2)}) async-start(bf16[8,128,256]{1,2,0:T(8,128)(2,1)} %bitcast.30), calls=%async_computation.3 | async-start | bytes 1048576 | tf_op jit(solution)/shard_map/all_to_all | solution.py:54
  61.0 12.5 %collective-permute-start.3 = (bf16[3,2,64,512]{3,2,1,0:T(8,128)(2,1)S(1)}, bf16[3,2,64,512]{3,2,1,0:T(8,128)(2,1)}, u32[]{:S(2)}, u32[]{:S(2)}) collective-permute-start(bf16[3,2,64,512]{3,2,1,0:T(8,128)(2,1)S(1)} %pad_maximum_fusion.3), channel_id=1, source_target_pairs={{0,16},{16,0},{32,48},{48,32},{1,17},{17,1},{33,49},{49,33},{2,18}... | collective-permute-start | bytes 1179656 | tf_op jit(solution)/shard_map/ppermute | solution.py:23
  64.2 20.0 %collective-permute-start.4 = (bf16[3,2,64,512]{3,2,1,0:T(8,128)(2,1)S(1)}, bf16[3,2,64,512]{3,2,1,0:T(8,128)(2,1)S(1)}, u32[]{:S(2)}, u32[]{:S(2)}) collective-permute-start(bf16[3,2,64,512]{3,2,1,0:T(8,128)(2,1)S(1)} %pad_maximum_fusion.3), channel_id=1, source_target_pairs={{0,32},{16,48},{32,0},{48,16},{1,33},{17,49},{33,1},{49,17},{2,34}... | collective-permute-start | bytes 1179656 | tf_op jit(solution)/shard_map/ppermute | solution.py:23
  68.6 21.5 %collective-permute-start.5 = (bf16[3,2,64,512]{3,2,1,0:T(8,128)(2,1)S(1)}, bf16[3,2,64,512]{3,2,1,0:T(8,128)(2,1)S(1)}, u32[]{:S(2)}, u32[]{:S(2)}) collective-permute-start(bf16[3,2,64,512]{3,2,1,0:T(8,128)(2,1)S(1)} %pad_maximum_fusion.3), channel_id=1, source_target_pairs={{0,48},{16,32},{32,16},{48,0},{1,49},{17,33},{33,17},{49,1},{2,50}... | collective-permute-start | bytes 1179656 | tf_op jit(solution)/shard_map/ppermute | solution.py:23
  74.6 18.8 %collective-permute-start.1 = (bf16[4,136,512]{2,1,0:T(8,128)(2,1)S(1)}, bf16[4,136,512]{2,1,0:T(8,128)(2,1)}, u32[]{:S(2)}, u32[]{:S(2)}) collective-permute-start(bf16[4,136,512]{2,1,0:T(8,128)(2,1)S(1)} %all-to-all-done), channel_id=1, source_target_pairs={{0,1},{1,0},{2,3},{3,2},{4,5},{5,4},{6,7},{7,6},{8,9},{9,8},{10,11... | collective-permute-start | bytes 1671176 | tf_op jit(solution)/shard_map/ppermute | solution.py:19
  91.5 13.8 %collective-permute-start.7 = (bf16[1024,256]{1,0:T(8,128)(2,1)S(1)}, bf16[1024,256]{1,0:T(8,128)(2,1)S(1)}, u32[]{:S(2)}, u32[]{:S(2)}) collective-permute-start(bf16[1024,256]{1,0:T(8,128)(2,1)S(1)} %bitcast.122), channel_id=1, source_target_pairs={{0,64},{64,0},{128,192},{192,128},{1,65},{65,1},{129,193},{193,129... | collective-permute-start | bytes 1572872 | tf_op jit(solution)/shard_map/ppermute | solution.py:23
  94.6 1.0 copy-start.2
  94.9 1.5 copy-start.1
  109.2 15.1 %collective-permute-start.8 = (bf16[392,512]{1,0:T(8,128)(2,1)}, bf16[392,512]{1,0:T(8,128)(2,1)}, u32[]{:S(2)}, u32[]{:S(2)}) collective-permute-start(bf16[392,512]{1,0:T(8,128)(2,1)} %get-tuple-element.17), channel_id=1, source_target_pairs={{0,16},{16,0},{32,48},{48,32},{1,17},{17,1},{33,49},{49,33},{2,18}... | collective-permute-start | bytes 1204232 | tf_op jit(solution)/shard_map/ppermute | solution.py:23
  111.1 20.6 %collective-permute-start.10 = (bf16[392,512]{1,0:T(8,128)(2,1)}, bf16[392,512]{1,0:T(8,128)(2,1)}, u32[]{:S(2)}, u32[]{:S(2)}) collective-permute-start(bf16[392,512]{1,0:T(8,128)(2,1)} %get-tuple-element.18), channel_id=1, source_target_pairs={{0,48},{16,32},{32,16},{48,0},{1,49},{17,33},{33,17},{49,1},{2,50}... | collective-permute-start | bytes 1204232 | tf_op jit(solution)/shard_map/ppermute | solution.py:23
  113.3 18.5 %collective-permute-start.9 = (bf16[392,512]{1,0:T(8,128)(2,1)}, bf16[392,512]{1,0:T(8,128)(2,1)}, u32[]{:S(2)}, u32[]{:S(2)}) collective-permute-start(bf16[392,512]{1,0:T(8,128)(2,1)} %get-tuple-element.19), channel_id=1, source_target_pairs={{0,32},{16,48},{32,0},{48,16},{1,33},{17,49},{33,1},{49,17},{2,34}... | collective-permute-start | bytes 1204232 | tf_op jit(solution)/shard_map/ppermute | solution.py:23
  120.1 39.0 %all-to-all-start.1 = ((bf16[4,128,1024]{2,1,0:T(8,128)(2,1)}), bf16[4,128,1024]{2,1,0:T(8,128)(2,1)}, u32[]{:S(2)}, u32[]{:S(2)}) async-start(bf16[4,128,1024]{2,1,0:T(8,128)(2,1)} %bitcast.121), calls=%async_computation.1 | async-start | bytes 2097152 | tf_op jit(solution)/shard_map/all_to_all | solution.py:112
  133.4 25.6 %collective-permute-start.11 = (bf16[200,512]{1,0:T(8,128)(2,1)S(1)}, bf16[200,512]{1,0:T(8,128)(2,1)S(1)}, u32[]{:S(2)}, u32[]{:S(2)}) collective-permute-start(bf16[200,512]{1,0:T(8,128)(2,1)S(1)} %pad_maximum_fusion.7), channel_id=1, source_target_pairs={{0,8},{8,0},{1,9},{9,1},{2,10},{10,2},{3,11},{11,3},{4,12},{12,4},... | collective-permute-start | bytes 614408 | tf_op jit(solution)/shard_map/ppermute | solution.py:19
  160.6 24.1 %collective-permute-start.6 = (bf16[64,1024]{1,0:T(8,128)(2,1)S(1)}, bf16[64,1024]{1,0:T(8,128)(2,1)S(1)}, u32[]{:S(2)}, u32[]{:S(2)}) collective-permute-start(bf16[64,1024]{1,0:T(8,128)(2,1)S(1)} %select_convert_fusion.1), channel_id=1, source_target_pairs={{0,256},{256,0},{1,257},{257,1},{2,258},{258,2},{3,259},{259,3},{4... | collective-permute-start | bytes 393224 | tf_op jit(solution)/shard_map/ppermute | solution.py:19
  185.4 9.9 %all-to-all-start.2 = ((bf16[8,64,128]{2,1,0:T(8,128)(2,1)}), bf16[8,64,128]{2,1,0:T(8,128)(2,1)S(1)}, u32[]{:S(2)}, u32[]{:S(2)}) async-start(bf16[8,64,128]{2,1,0:T(8,128)(2,1)} %copy.39), calls=%async_computation.2 | async-start | bytes 262144 | tf_op jit(solution)/shard_map/all_to_all | solution.py:119
